TPU v7x, 32 devices: a whole 2x2x4 slice. The times are simulated.
32 devices in a mesh: dp: 16 (over z, x, core), tensor: 2 (over y).
Axes of the slice: x: 2, y: 2, z: 4, core: 2. Of those that a mesh axis runs over, the one named last changes fastest.
Arguments:
- tokens: bfloat16 [16, 1024, 1536], P('dp', 'tensor'), may hold values from -6 to 6
- segment_ids: int32 [16, 1024], P('dp'), may hold values from 0 to 5, as said below
- positions: int32 [16, 1024], P('dp'), may hold values from 0 to 1023, as said below
- query_weight: float32 [1536, 1536], P('dp', 'tensor'), may hold values from -0.15625 to 0.15625
- key_master_weight: float32 [1536, 768], P('dp', 'tensor'), may hold values from -0.15625 to 0.15625
- value_master_weight: float32 [1536, 768], P('dp', 'tensor'), may hold values from -0.15625 to 0.15625
- out_weight: float32 [1536, 1536], P('tensor', 'dp'), may hold values from -1.25 to 1.25
- attn_gain: float32 [1536], P('dp'), may hold values from 0.5 to 1.5
- gate_weight: float32 [1536, 4096], P('dp', 'tensor'), may hold values from -0.15625 to 0.15625
- up_weight: float32 [1536, 4096], P('dp', 'tensor'), may hold values from -0.15625 to 0.15625
- down_weight: float32 [4096, 1536], P('tensor', 'dp'), may hold values from -0.09375 to 0.09375
- mlp_gain: float32 [1536], P('dp'), may hold values from 0.5 to 1.5
- cotangent: bfloat16 [16, 1024, 1536], P('dp', 'tensor'), may hold values from -8 to 8
Outputs:
- output: bfloat16 [16, 1024, 1536], P('dp', 'tensor')
- input_grad: bfloat16 [16, 1024, 1536], P('dp', 'tensor')
- grad_query_weight: float32 [1536, 1536], P('dp', 'tensor')
- grad_key_weight: float32 [1536, 768], P('dp', 'tensor')
- grad_value_weight: float32 [1536, 768], P('dp', 'tensor')
- grad_out_weight: float32 [1536, 1536], P('tensor', 'dp')
- grad_attn_gain: float32 [1536], P('dp')
- grad_gate_weight: float32 [1536, 4096], P('dp', 'tensor')
- grad_up_weight: float32 [1536, 4096], P('dp', 'tensor')
- grad_down_weight: float32 [4096, 1536], P('tensor', 'dp')
- grad_mlp_gain: float32 [1536], P('dp')
Inputs may be any that keep to these rules, and one draw needn't show every extreme that they name: `segment_ids`: along each sequence the ids start at 0 and rise by one at the first token of each document; every document except a sequence's last holds at least 204 tokens. `positions`: each token's place within its document: 0 at a document's first token, rising by one along it.
All inputs are finite; a program needn't handle non-finite values.
Results may differ from a plain program's by a relative error of at most 0.018.
Values may be sent and summed in bfloat16 or wider, within the bound.
No kernel may reach another device: no remote copies, remote signals or barrier semaphores. Data moves between devices by JAX's collectives and lax.ppermute only.
A program may use at most 192 MiB of HBM per device.

v0:
```python
import functools
import math

import jax
import jax.numpy as jnp
from jax import lax
from jax.experimental import pallas as pl
from jax.experimental.pallas import tpu as pltpu
from jax.sharding import PartitionSpec as P

HEAD_DIM = 96
PAD_DIM = 128
BLOCK = 256
DOCS = 16
EPSILON = 1e-05
ROPE_BASE = 100000.0
FAR = float(2**30)
RING_LIMIT = 16
TILE = 512
VMEM = 66_000_000
SCALE = 1.0 / math.sqrt(HEAD_DIM)
LOG2E = math.log2(math.e)

F32 = jnp.float32
BF16 = jnp.bfloat16


def mm(left, right, left_dim, right_dim, dtype=F32):
    return lax.dot_general(
        left, right, (((left_dim,), (right_dim,)), ((), ())), preferred_element_type=F32
    ).astype(dtype)


def swap_halves(value):
    return lax.ppermute(value, "tensor", [(0, 1), (1, 0)])


def is_ring(dp):
    return 8 <= dp <= RING_LIMIT and dp & (dp - 1) == 0


def chip_of(spot, chips):
    return jnp.where(2 * spot < chips, 2 * spot, 2 * (chips - 1 - spot) + 1)


def ring_pairs(dp):
    chips = dp // 2
    order = list(range(0, chips, 2)) + list(range(chips - 1, 0, -2))
    ahead = []
    for spot in range(chips):
        here, following = order[spot], order[(spot + 1) % chips]
        ahead += [(2 * here, 2 * following), (2 * here + 1, 2 * following + 1)]
    return ahead, [(b, a) for a, b in ahead]


def ring_place(dp):
    chips = dp // 2
    me = lax.axis_index("dp").astype(jnp.int32)
    chip = me >> 1
    return me & 1, jnp.where(chip & 1 == 0, chip >> 1, chips - 1 - (chip >> 1))


def piece_steps(dp):
    reach = dp // 4
    return [0, *range(-1, -reach, -1), *range(1, reach), reach, reach]


def piece_blocks(dp):
    if not is_ring(dp):
        return jnp.zeros((1,), jnp.int32)
    chips = dp // 2
    core, spot = ring_place(dp)
    chip = chip_of((spot + jnp.asarray(piece_steps(dp), jnp.int32)) & (chips - 1), chips)
    return jnp.concatenate([2 * chip + core, 2 * chip + 1 - core])


def turn_blocks(dp):
    if not is_ring(dp):
        return jnp.zeros((1,), jnp.int32)
    chips = dp // 2
    core, spot = ring_place(dp)
    chip = chip_of((spot + jnp.arange(chips, dtype=jnp.int32)) & (chips - 1), chips)
    return jnp.concatenate([2 * chip + 1 - core, 2 * chip + core])


class Order:
    def __init__(self, flag):
        self.token = lax.create_token()
        self.flag = flag

    def tie(self, *values):
        tied = lax.optimization_barrier((self.token, *values))[1:]
        return tied if len(values) > 1 else tied[0]

    def done(self, *values):
        self.token, *values = lax.optimization_barrier((self.token, *values))
        return values if len(values) > 1 else values[0]


class Gather:
    def __init__(self, shard, dp, cut):
        self.dp, self.cut = dp, cut
        self.behind, self.ahead, self.other, self.shard = [], [], [], shard

    def share(self, order):
        if not is_ring(self.dp):
            return
        found = (self.behind[-1], self.ahead[-1]) if self.other else (self.shard,)
        swap = [(i, i ^ 1) for i in range(self.dp)]

        def both(*pieces):
            return tuple(lax.ppermute(piece, "dp", swap) for piece in pieces)

        def neither(*pieces):
            return tuple(jnp.zeros_like(piece) for piece in pieces)

        found = order.tie(*found) if len(found) > 1 else (order.tie(*found),)
        got = lax.cond(order.flag, both, neither, *found)
        self.other.append(order.done(*got) if len(got) > 1 else [order.done(*got)])

    def round(self, order):
        if not is_ring(self.dp):
            return
        forth, back = ring_pairs(self.dp)
        left = self.behind[-1] if self.behind else self.shard
        right = self.ahead[-1] if self.ahead else self.shard
        left, right = order.tie(left, right)
        if len(self.behind) == self.dp // 4 - 1:
            left, right = halves(left, right, self.cut)
        left, right = order.done(left, right)
        self.behind.append(lax.ppermute(left, "dp", forth))
        self.ahead.append(lax.ppermute(right, "dp", back))

    def arrive(self, order):
        if is_ring(self.dp):
            self.behind[-1], self.ahead[-1] = order.done(self.behind[-1], self.ahead[-1])

    def next(self, order):
        if not is_ring(self.dp):
            return
        self.arrive(order)
        arrived = self.behind[-1], self.ahead[-1]
        self.round(order)
        sent = self.behind.pop(), self.ahead.pop()
        self.behind[-1], self.ahead[-1] = arrived
        self.share(order)
        self.behind.append(sent[0])
        self.ahead.append(sent[1])

    def pieces(self, order):
        if not is_ring(self.dp):
            return [(lax.all_gather(self.shard, "dp", axis=0, tiled=True), 0)]
        self.arrive(order)
        self.share(order)
        held = [self.shard, *self.behind[:-1], *self.ahead[:-1], self.behind[-1], self.ahead[-1]]
        other = [self.other[0][0], *(pair[0] for pair in self.other[1:-1])]
        other += [*(pair[1] for pair in self.other[1:-1]), *self.other[-1]]
        columns = [0] * (len(held) - 1) + [self.cut]
        return list(zip([*held, *other], columns * 2))


class Scatter:
    def __init__(self, dp, order, *columns):
        self.dp, self.order = dp, order
        lefts, rights, dims = zip(*columns)
        rights = order.tie(*rights) if len(rights) > 1 else (order.tie(*rights),)
        if not is_ring(dp):
            full = order.done(products(0, 1, lefts, rights, dims))
            self.total = lax.psum_scatter(full, "dp", scatter_dimension=0, tiled=True).astype(F32)
            return
        self.chips = dp // 2
        self.reach = self.chips // 2
        self.rows = lefts[0].shape[0] // dp

        def both(lefts, rights):
            token = lax.create_token()
            theirs = products(0, 2, lefts, rights, dims)
            token, theirs = lax.optimization_barrier((token, theirs))
            got = lax.ppermute(theirs, "dp", [(i, i ^ 1) for i in range(dp)])
            rights = lax.optimization_barrier((token, *rights))[1:]
            return got, products(1, 2, lefts, rights, dims)

        def neither(lefts, rights):
            width = sum(right.shape[1 - dim] for right, dim in zip(rights, dims))
            return (jnp.zeros((lefts[0].shape[0] // 2, width), BF16),) * 2

        self.got, self.mine = order.done(*lax.cond(order.flag, both, neither, lefts, tuple(rights)))
        self.width = self.mine.shape[1]
        self.ahead = self.behind = None

    def local(self, steps, mine, first, low_edge, high_edge):
        block = steps % self.chips
        return [(part, block, first, low_edge, high_edge) for part in (mine, self.got)]

    def round(self):
        if not is_ring(self.dp):
            return
        forth, back = ring_pairs(self.dp)
        half = self.width // 2
        tile = half if half <= 1536 else half // 2
        count = half // tile
        mine = self.order.tie(self.mine)
        reach = self.reach
        if self.ahead is None:
            right = self.local(reach, mine, 0, 0, count)
            left = self.local(reach, mine, count, 0, count)
        else:
            cut = count if self.ahead.shape[1] == half else 2 * count
            right = [*self.local(reach, mine, 0, 0, 2 * count), (self.ahead, 0, 0, 0, cut)]
            left = [*self.local(-reach, mine, 0, 0, 2 * count)]
            left.append((self.behind, 0, 0, 2 * count - cut, 2 * count))
        right, left = self.order.done(*combine(self.rows, tile, [right, left]))
        self.ahead = lax.ppermute(right, "dp", forth)
        self.behind = lax.ppermute(left, "dp", back)
        self.reach -= 1

    def result(self, pieces, weights):
        if not is_ring(self.dp):
            parts = [self.total] + [jnp.zeros_like(self.total)] * 3
        else:
            parts = [self.order.tie(self.mine), self.got, self.ahead, self.behind]
        return self.order.done(*finish(parts, [0] * 4, pieces, weights))


def rope_rows(top, bottom, cos, sin):
    return top * cos - bottom * sin, bottom * cos + top * sin


def project_kernel(columns, rows, heads, block_ref, turn_ref, own_ref, par_ref, cos_ref, sin_ref, *rest):
    count = len(columns)
    pieces = rest[:count]
    qkv_ref, gain_ref, at_ref, wide_ref, out_ref = rest[count : count + 5]
    w_scr, a_scr, at_scr, in_sem, out_sem, turn_sem = rest[count + 5 :]
    step = pl.program_id(0)
    tiles = pl.num_programs(0)
    own_rows, model = own_ref.shape
    tile = qkv_ref.shape[0]
    half = HEAD_DIM // 2
    qkv_width = 2 * heads

    def loads(i):
        base = pl.multiple_of(block_ref[i] * rows, rows)
        place = slice(columns[i], columns[i] + pieces[i].shape[1])
        return pltpu.make_async_copy(pieces[i], w_scr.at[pl.ds(base, rows), place], in_sem.at[i])

    def stores():
        return (
            pltpu.make_async_copy(w_scr.at[:, :qkv_width], wide_ref, out_sem.at[0]),
            pltpu.make_async_copy(
                w_scr.at[:, qkv_width : qkv_width + heads], out_ref, out_sem.at[1]
            ),
        )

    def turns(i):
        block = model // turn_ref.shape[0]
        base = pl.multiple_of(turn_ref[i] * block, block)
        return pltpu.make_async_copy(
            at_scr.at[pl.ds(base, block), :], at_ref.at[pl.ds(i * block, block), :], turn_sem.at[i]
        )

    @pl.when(step == 0)
    def _():
        for i in range(count):
            loads(i).start()
        for i in range(count):
            loads(i).wait()
        gains = w_scr[:, qkv_width + heads :].astype(F32).T
        gain_ref[...] = gains[:8, :]
        gain = gains[:1, :]
        for number, ref in enumerate((own_ref, par_ref)):

            @pl.loop(0, own_rows // BLOCK)
            def _(part, ref=ref, number=number):
                start = pl.multiple_of(part * BLOCK, BLOCK)
                x = ref[pl.ds(start, BLOCK), :].astype(F32)
                inverse = lax.rsqrt(jnp.mean(x * x, -1, keepdims=True) + EPSILON)
                normed = x * inverse * gain
                place = pl.multiple_of(start + number * own_rows, BLOCK)
                a_scr[pl.ds(place, BLOCK), :] = normed.astype(BF16)
                at_scr[:, pl.ds(place, BLOCK)] = normed.T.astype(BF16)

        for copy in stores():
            copy.start()
        for i in range(turn_ref.shape[0]):
            turns(i).start()

    start = pl.multiple_of(step * tile, 128)
    flat = mm(a_scr[...], w_scr[:, pl.ds(start, tile)], 1, 0).T

    @pl.when(step < tiles - tiles // 4)
    def _():
        cos, sin = cos_ref[...], sin_ref[...]
        for h in range(tile // HEAD_DIM):
            base = h * HEAD_DIM
            top, bottom = rope_rows(
                flat[base : base + half, :], flat[base + half : base + HEAD_DIM, :], cos, sin
            )
            qkv_ref[base : base + half, :] = top.astype(BF16)
            qkv_ref[base + half : base + HEAD_DIM, :] = bottom.astype(BF16)

    @pl.when(step >= tiles - tiles // 4)
    def _():
        qkv_ref[...] = flat.astype(BF16)

    @pl.when(step == tiles - 1)
    def _():
        for copy in stores():
            copy.wait()
        for i in range(turn_ref.shape[0]):
            turns(i).wait()


FREE = pl.CostEstimate(flops=0, bytes_accessed=0, transcendentals=0)
LONG = pl.CostEstimate(flops=0, bytes_accessed=40 * 2**20, transcendentals=0)


def product_kernel(left_ref, right_ref, *out_refs):
    half = left_ref.shape[0] // 2

    @pl.loop(0, 2)
    def _(part):
        start = pl.multiple_of(part * half, half)
        out = mm(left_ref[pl.ds(start, half), :], right_ref[...], 1, 1, BF16)
        for number, ref in enumerate(out_refs):

            @pl.when(part == number)
            def _(ref=ref):
                ref[...] = out


def product(left, right):
    rows, depth = left.shape
    width = right.shape[0]
    tile = next(t for t in (TILE, 384, 256, width) if width % t == 0)
    spec = pl.BlockSpec
    return pl.pallas_call(
        product_kernel,
        grid=(width // tile,),
        in_specs=[spec((rows, depth), lambda j: (0, 0)), spec((tile, depth), lambda j: (j, 0))],
        out_specs=[spec((rows // 2, tile), lambda j: (0, j))] * 2,
        out_shape=[jax.ShapeDtypeStruct((rows // 2, width), BF16)] * 2,
        compiler_params=pltpu.CompilerParams(vmem_limit_bytes=VMEM),
        cost_estimate=FREE,
        name="product",
    )(left, right)


def products_kernel(starts, dims, *refs):
    count = len(dims)
    out_ref = refs[-1]
    step = pl.program_id(0)
    for i, dim in enumerate(dims):

        @pl.when((step >= starts[i]) & (step < starts[i + 1]))
        def _(i=i, dim=dim):
            width = out_ref.shape[1]
            size = TILE if width % TILE == 0 else width

            @pl.loop(0, width // size)
            def _(j):
                place = pl.ds(pl.multiple_of(j * size, 128), size)
                right = refs[count + i][place, :] if dim else refs[count + i][:, place]
                out_ref[:, place] = mm(refs[i][...], right, 1, dim, out_ref.dtype)


def products(part, parts, lefts, rights, dims):
    rows, depth = lefts[0].shape
    rows = rows // parts
    widths = [right.shape[1 - dim] for right, dim in zip(rights, dims)]
    tile = next(t for t in (1024, 768, TILE, 384) if all(width % t == 0 for width in widths))
    starts = [0]
    for width in widths:
        starts.append(starts[-1] + width // tile)
    spec = pl.BlockSpec
    in_specs = [spec((rows, depth), lambda j: (part, 0)) for _ in lefts]
    for i, dim in enumerate(dims):

        def place(j, i=i):
            return jnp.clip(j - starts[i], 0, starts[i + 1] - starts[i] - 1)

        if dim:
            in_specs.append(spec((tile, depth), lambda j, place=place: (place(j), 0)))
        else:
            in_specs.append(spec((depth, tile), lambda j, place=place: (0, place(j))))
    return pl.pallas_call(
        functools.partial(products_kernel, starts, dims),
        grid=(starts[-1],),
        in_specs=in_specs,
        out_specs=spec((rows, tile), lambda j: (0, j)),
        out_shape=jax.ShapeDtypeStruct((rows, sum(widths)), BF16),
        compiler_params=pltpu.CompilerParams(vmem_limit_bytes=VMEM),
        cost_estimate=FREE,
        name="products",
    )(*lefts, *rights)


def turned_kernel(left_ref, right_ref, out_ref):
    out_ref[...] = mm(left_ref[...], right_ref[...], 1, 0).T.astype(BF16)


def turned_product(left, right, tile, start=0, count=None):
    rows, depth = left.shape
    count = count or right.shape[1] // tile
    spec = pl.BlockSpec
    return pl.pallas_call(
        turned_kernel,
        grid=(count,),
        in_specs=[
            spec((rows, depth), lambda j: (0, 0)),
            spec((depth, tile), lambda j: (0, start + j)),
        ],
        out_specs=spec((tile, rows), lambda j: (j, 0)),
        out_shape=jax.ShapeDtypeStruct((count * tile, rows), BF16),
        compiler_params=pltpu.CompilerParams(vmem_limit_bytes=VMEM),
        cost_estimate=FREE,
        name="turned_product",
    )(left, right)


def join_kernel(*refs):
    start = 0
    for ref in refs[:-1]:
        refs[-1][:, start : start + ref.shape[1]] = ref[...].astype(BF16)
        start += ref.shape[1]


def join(*parts):
    rows = parts[0].shape[0]
    return pl.pallas_call(
        join_kernel,
        out_shape=jax.ShapeDtypeStruct((rows, sum(part.shape[1] for part in parts)), BF16),
        compiler_params=pltpu.CompilerParams(vmem_limit_bytes=VMEM),
        cost_estimate=FREE,
        name="join",
    )(*parts)


def halves_kernel(cut, left_ref, right_ref, low_ref, high_ref):
    low_ref[...] = left_ref[:, :cut]
    high_ref[...] = right_ref[:, cut:]


def halves(left, right, cut):
    rows, width = left.shape
    return pl.pallas_call(
        functools.partial(halves_kernel, cut),
        out_shape=[
            jax.ShapeDtypeStruct((rows, cut), left.dtype),
            jax.ShapeDtypeStruct((rows, width - cut), left.dtype),
        ],
        compiler_params=pltpu.CompilerParams(vmem_limit_bytes=VMEM),
        cost_estimate=FREE,
        name="halves",
    )(left, right)


def residual_kernel(part_ref, sent_ref, x_ref, gain_ref, middle_ref, b_ref):
    middle = x_ref[...].astype(F32) + (part_ref[...] + sent_ref[...].astype(F32))
    inverse = lax.rsqrt(jnp.mean(middle * middle, -1, keepdims=True) + EPSILON)
    middle_ref[...] = middle
    b_ref[...] = (middle * inverse * gain_ref[1:2, :]).astype(BF16)


def back_kernel(row, own_ref, sent_ref, value_ref, base_ref, gain_ref, *out_refs):
    upstream = own_ref[...].astype(F32) + sent_ref[...].astype(F32)
    value = value_ref[...].astype(F32)
    inverse = lax.rsqrt(jnp.mean(value * value, -1, keepdims=True) + EPSILON)
    scaled = upstream * gain_ref[row : row + 1, :]
    inner = jnp.mean(scaled * value, -1, keepdims=True)
    out = inverse * (scaled - value * (inverse * inverse * inner))
    out = base_ref[...].astype(F32) + out
    for ref in out_refs:
        ref[...] = out.astype(ref.dtype)


def by_rows(kernel, arrays, gain, dtypes, name):
    rows, width = arrays[0].shape
    step = 128
    block = pl.BlockSpec((step, width), lambda i: (i, 0))
    return pl.pallas_call(
        kernel,
        grid=(rows // step,),
        in_specs=[block] * len(arrays) + [pl.BlockSpec(gain.shape, lambda i: (0, 0))],
        out_specs=[block] * len(dtypes),
        out_shape=[jax.ShapeDtypeStruct((rows, width), dtype) for dtype in dtypes],
        compiler_params=pltpu.CompilerParams(vmem_limit_bytes=VMEM),
        cost_estimate=FREE,
        name=name,
    )(*arrays, gain)


def finish_kernel(pieces, weighted, *refs):
    parts, refs = refs[:4], refs[4:]
    weights, refs = refs[:weighted], refs[weighted:]
    outs, gain_ref, total_ref = refs[: len(pieces)], refs[-2], refs[-1]
    total_ref[...] = jnp.zeros_like(total_ref)
    for number, (out_ref, (start, size, stride, steps)) in enumerate(zip(outs, pieces)):

        @pl.loop(0, steps)
        def _(j, number=number, out_ref=out_ref, start=start, size=size, stride=stride):
            source = pl.ds(pl.multiple_of(start + j * stride, 128), size)
            target = pl.ds(pl.multiple_of(j * size, 128), size)
            total = sum(part[:, source].astype(F32) for part in parts)
            out_ref[:, target] = total
            if number < weighted:
                total = total * weights[number][:, target].astype(BF16).astype(F32)
                for k in range(0, size, 128):
                    total_ref[...] += total[:, k : k + 128]

    rows = jnp.broadcast_to(jnp.sum(total_ref[...], 1, keepdims=True), total_ref.shape)
    gain_ref[...] = rows.T[:8, :]


def finish(parts, blocks, pieces, weights):
    rows = weights[0].shape[0]
    width = parts[0].shape[1]
    spec = pl.BlockSpec
    whole = lambda i: (0, 0)
    widths = [size * steps for _, size, _, steps in pieces]
    return pl.pallas_call(
        functools.partial(finish_kernel, pieces, len(weights)),
        grid=(1,),
        in_specs=[spec((rows, width), lambda i, block=block: (block, 0)) for block in blocks]
        + [spec(weight.shape, whole) for weight in weights],
        out_specs=[spec((rows, size), whole) for size in widths] + [spec((8, rows), whole)],
        out_shape=[jax.ShapeDtypeStruct((rows, size), F32) for size in widths]
        + [jax.ShapeDtypeStruct((8, rows), F32)],
        scratch_shapes=[pltpu.VMEM((rows, 128), F32)],
        compiler_params=pltpu.CompilerParams(vmem_limit_bytes=VMEM),
        cost_estimate=FREE,
        name="finish",
    )(*parts, *weights)


def combine_kernel(outs, *refs):
    step = pl.program_id(0)
    inputs = list(refs[: -len(outs)])
    for out_ref, terms in zip(refs[-len(outs) :], outs):
        total = None
        for low_edge, high_edge in terms:
            value = inputs.pop(0)[...].astype(F32)
            if high_edge - low_edge < pl.num_programs(0):
                value = jnp.where((step >= low_edge) & (step < high_edge), value, 0.0)
            total = value if total is None else total + value
        out_ref[...] = total.astype(out_ref.dtype)


def combine(rows, tile, outs, dtype=BF16):
    tiles = max(high for terms in outs for *_, high in terms)
    in_specs, arrays, edges = [], [], []
    for terms in outs:
        edges.append([(low_edge, high_edge) for *_, low_edge, high_edge in terms])
        for array, block, first, low_edge, high_edge in terms:

            def place(j, block=block, first=first, low_edge=low_edge, high_edge=high_edge):
                return block, jnp.clip(j, low_edge, high_edge - 1) - low_edge + first

            in_specs.append(pl.BlockSpec((rows, tile), place))
            arrays.append(array)
    return pl.pallas_call(
        functools.partial(combine_kernel, edges),
        grid=(tiles,),
        in_specs=in_specs,
        out_specs=[pl.BlockSpec((rows, tile), lambda j: (0, j)) for _ in outs],
        out_shape=[jax.ShapeDtypeStruct((rows, tiles * tile), dtype) for _ in outs],
        compiler_params=pltpu.CompilerParams(vmem_limit_bytes=VMEM),
        cost_estimate=FREE,
        name="combine",
    )(*arrays)


def turn_kernel(turn_ref, own_ref, par_ref, out_ref, scr):
    own_rows, model = own_ref.shape
    step = BLOCK // 2
    for number, ref in enumerate((own_ref, par_ref)):

        @pl.loop(0, own_rows // step)
        def _(part, ref=ref, number=number):
            start = pl.multiple_of(part * step, step)
            place = pl.multiple_of(start + number * own_rows, step)
            scr[:, pl.ds(place, step)] = ref[pl.ds(start, step), :].astype(F32).T.astype(BF16)

    count = turn_ref.shape[0]
    block = model // count

    @pl.loop(0, count)
    def _(i):
        base = pl.multiple_of(turn_ref[i] * block, block)
        place = pl.multiple_of(i * block, block)
        out_ref[pl.ds(place, block), :] = scr[pl.ds(base, block), :]


def turn(turned, own, par):
    own_rows, model = own.shape
    length = 2 * own_rows
    whole = lambda i, t: (0, 0)
    spec = pl.BlockSpec
    return pl.pallas_call(
        turn_kernel,
        grid_spec=pltpu.PrefetchScalarGridSpec(
            num_scalar_prefetch=1,
            grid=(1,),
            in_specs=[spec((own_rows, model), whole)] * 2,
            out_specs=spec((model, length), whole),
            scratch_shapes=[pltpu.VMEM((model, length), BF16)],
        ),
        out_shape=jax.ShapeDtypeStruct((model, length), BF16),
        compiler_params=pltpu.CompilerParams(vmem_limit_bytes=VMEM),
        cost_estimate=LONG,
        name="turn",
    )(turned, own, par)


def project(blocks, turned, x_own, x_par, cos, sin, pieces, heads):
    own_rows, model = x_own.shape
    length = 2 * own_rows
    count = len(pieces)
    columns = [column for _, column in pieces]
    pieces = [piece for piece, _ in pieces]
    rows, width = pieces[0].shape
    qkv_width = 2 * heads
    tile = heads // 2
    spec = pl.BlockSpec
    whole = lambda j, s, t: (0, 0)
    anywhere = spec(memory_space=pl.ANY)
    return pl.pallas_call(
        functools.partial(project_kernel, columns, rows, heads),
        grid_spec=pltpu.PrefetchScalarGridSpec(
            num_scalar_prefetch=2,
            grid=(qkv_width // tile,),
            in_specs=[
                spec((own_rows, model), whole),
                spec((own_rows, model), whole),
                spec((HEAD_DIM // 2, length), whole),
                spec((HEAD_DIM // 2, length), whole),
            ]
            + [anywhere] * count,
            out_specs=[
                spec((tile, length), lambda j, s, t: (j, 0)),
                spec((8, model), whole),
                anywhere,
                anywhere,
                anywhere,
            ],
            scratch_shapes=[
                pltpu.VMEM((model, width), BF16),
                pltpu.VMEM((length, model), BF16),
                pltpu.VMEM((model, length), BF16),
                pltpu.SemaphoreType.DMA((count,)),
                pltpu.SemaphoreType.DMA((2,)),
                pltpu.SemaphoreType.DMA(turned.shape),
            ],
        ),
        out_shape=[
            jax.ShapeDtypeStruct((qkv_width, length), BF16),
            jax.ShapeDtypeStruct((8, model), F32),
            jax.ShapeDtypeStruct((model, length), BF16),
            jax.ShapeDtypeStruct((model, qkv_width), BF16),
            jax.ShapeDtypeStruct((model, heads), BF16),
        ],
        compiler_params=pltpu.CompilerParams(vmem_limit_bytes=VMEM),
        cost_estimate=FREE,
        name="project",
    )(blocks, turned, x_own, x_par, cos, sin, *pieces)


def ffn_kernel(columns, rows, ff, block_ref, b_own, b_par, e_own, e_par, *rest):
    count = len(columns)
    pieces = rest[:count]
    hidden_ref, pair_ref, own_ref, par_ref, down_ref = rest[count : count + 5]
    b_scr, e_scr, w_scr, total, sem, save_sem = rest[count + 5 :]
    step = pl.program_id(0)
    tiles = pl.num_programs(0)
    slot = lax.rem(step, 2)
    width = hidden_ref.shape[1]
    half = b_own.shape[0]

    def fetch(number, into):
        for kind in range(3):
            for i in range(count):
                base = pl.multiple_of(block_ref[i] * rows, rows)
                column = pl.multiple_of(kind * ff + number * width, 128)
                low_edge, high_edge = columns[i], columns[i] + pieces[i].shape[1]

                def start(i=i, base=base, column=column, kind=kind):
                    pltpu.make_async_copy(
                        pieces[i].at[:, pl.ds(pl.multiple_of(column - columns[i], 128), width)],
                        w_scr.at[into, pl.ds(base, rows), kind * width : (kind + 1) * width],
                        sem.at[into],
                    ).start()

                if low_edge <= kind * ff and (kind + 1) * ff <= high_edge:
                    start()
                elif low_edge < (kind + 1) * ff and kind * ff < high_edge:
                    pl.when((column >= low_edge) & (column < high_edge))(start)

    def saved(number, source):
        column = pl.multiple_of(number * width, 128)
        return pltpu.make_async_copy(
            w_scr.at[source, :, 2 * width :], down_ref.at[:, pl.ds(column, width)], save_sem.at[source]
        )

    @pl.when(step == 0)
    def _():
        fetch(0, 0)
        for target, own, par in ((b_scr, b_own, b_par), (e_scr, e_own, e_par)):
            target[:half, :] = own[...]
            target[half:, :] = par[...]

    @pl.when(step > 0)
    def _():
        saved(step - 1, 1 - slot).wait()

    @pl.when(step + 1 < tiles)
    def _():
        fetch(step + 1, 1 - slot)

    pltpu.make_async_copy(w_scr.at[slot], w_scr.at[slot], sem.at[slot]).wait()
    saved(step, slot).start()
    first = mm(b_scr[...], w_scr[slot, :, : 2 * width], 1, 0)
    gate, up = first[:, :width], first[:, width:]
    dhid = mm(e_scr[...], w_scr[slot, :, 2 * width :], 1, 0)
    sig = 1.0 / (1.0 + jnp.exp(-gate))
    silu = gate * sig
    hidden_ref[...] = (silu * up).astype(BF16)
    dgate = (dhid * up * (sig * (1.0 + gate * (1.0 - sig)))).astype(BF16)
    dup = (dhid * silu).astype(BF16)
    pair_ref[:, :width] = dgate
    pair_ref[:, width:] = dup
    part = mm(pair_ref[...], w_scr[slot, :, : 2 * width], 1, 1)

    @pl.when(step == 0)
    def _():
        total[...] = part

    @pl.when((step > 0) & (step < tiles - 1))
    def _():
        total[...] += part

    @pl.when(step == tiles - 1)
    def _():
        own_ref[...] = total[:half, :] + part[:half, :]
        par_ref[...] = (total[half:, :] + part[half:, :]).astype(BF16)
        saved(step, slot).wait()


def ffn(blocks, b_own, b_par, e_own, e_par, pieces):
    half, model = b_own.shape
    count = len(pieces)
    columns = [column for _, column in pieces]
    pieces = [piece for piece, _ in pieces]
    rows = pieces[0].shape[0]
    ff = max(piece.shape[1] + column for piece, column in zip(pieces, columns)) // 3
    spec = pl.BlockSpec
    whole = lambda j, s: (0, 0)
    anywhere = spec(memory_space=pl.ANY)
    once = spec((half, model), whole, pipeline_mode=pl.Buffered(1))
    return pl.pallas_call(
        functools.partial(ffn_kernel, columns, rows, ff),
        grid_spec=pltpu.PrefetchScalarGridSpec(
            num_scalar_prefetch=1,
            grid=(ff // TILE,),
            in_specs=[once] * 4 + [anywhere] * count,
            out_specs=[
                spec((2 * half, TILE), lambda j, s: (0, j)),
                spec((2 * half, 2 * TILE), lambda j, s: (0, j)),
                once,
                once,
                anywhere,
            ],
            scratch_shapes=[
                pltpu.VMEM((2 * half, model), BF16),
                pltpu.VMEM((2 * half, model), BF16),
                pltpu.VMEM((2, model, 3 * TILE), BF16),
                pltpu.VMEM((2 * half, model), F32),
                pltpu.SemaphoreType.DMA((2,)),
                pltpu.SemaphoreType.DMA((2,)),
            ],
        ),
        out_shape=[
            jax.ShapeDtypeStruct((2 * half, ff), BF16),
            jax.ShapeDtypeStruct((2 * half, 2 * ff), BF16),
            jax.ShapeDtypeStruct((half, model), F32),
            jax.ShapeDtypeStruct((half, model), BF16),
            jax.ShapeDtypeStruct((model, ff), BF16),
        ],
        compiler_params=pltpu.CompilerParams(vmem_limit_bytes=VMEM),
        cost_estimate=FREE,
        name="ffn",
    )(blocks, b_own, b_par, e_own, e_par, *pieces)


def place_of(natural, side, length):
    return pl.multiple_of((natural + side * (length // 2)) & (length - 1), BLOCK)


def diagonal():
    keys = lax.broadcasted_iota(jnp.int32, (BLOCK, BLOCK), 0)
    queries = lax.broadcasted_iota(jnp.int32, (BLOCK, BLOCK), 1)
    return keys <= queries


def fill(scratch, rows, side, docs):
    length = rows.shape[1]
    half = length // 2
    scratch[HEAD_DIM:, :] = jnp.zeros((PAD_DIM - HEAD_DIM, length), BF16)
    if docs is not None:
        scratch[HEAD_DIM : HEAD_DIM + DOCS, :] = docs[...]
    for part in range(2):
        there = pl.ds(place_of(part * half, side, length), half)
        scratch[:HEAD_DIM, part * half : (part + 1) * half] = rows[:, there]


def forward_kernel(
    side_ref, q_in, k_in, v_in, oq_ref, ok_ref, *rest
):
    att_ref, lse_ref, q_scr, kt_scr, k_scr, v_scr = rest[-6:]
    length = q_in.shape[1]
    side = side_ref[0]
    blocks = length // BLOCK
    fill(kt_scr, k_in, side, ok_ref)
    fill(v_scr, v_in, side, None)
    k_scr[...] = kt_scr[...].T
    causal = diagonal()
    for h in range(2):
        rows = slice(h * HEAD_DIM, (h + 1) * HEAD_DIM)
        fill(q_scr, q_in.at[rows, :], side, oq_ref)
        for b in range(blocks):
            here = pl.ds(b * BLOCK, BLOCK)
            keys = (b + 1) * BLOCK
            query = q_scr[:, here]
            last = mm(k_scr[b * BLOCK : keys, :], query, 1, 0)
            last = jnp.where(causal, last, -FAR)
            top = jnp.max(last, 0, keepdims=True)
            if b:
                early = mm(k_scr[: b * BLOCK, :], query, 1, 0)
                top = jnp.maximum(top, jnp.max(early, 0, keepdims=True))
            top = top * (SCALE * LOG2E)
            weight = jnp.exp2(last * (SCALE * LOG2E) - top)
            total = jnp.sum(weight, 0, keepdims=True)
            out = mm(v_scr[:HEAD_DIM, b * BLOCK : keys], weight.astype(BF16), 1, 0)
            if b:
                weight = jnp.exp2(early * (SCALE * LOG2E) - top)
                total = total + jnp.sum(weight, 0, keepdims=True)
                out = out + mm(v_scr[:HEAD_DIM, : b * BLOCK], weight.astype(BF16), 1, 0)
            out = out / total
            there = pl.ds(place_of(b * BLOCK, side, length), BLOCK)
            att_ref[rows, there] = out.astype(BF16)
            lse_ref[0, h : h + 1, here] = top + jnp.log2(total)


def group_specs(groups, length):
    spec = pl.BlockSpec
    return [
        spec((2 * HEAD_DIM, length), lambda g, s: (g, 0)),
        spec((HEAD_DIM, length), lambda g, s: (2 * groups + g, 0)),
        spec((HEAD_DIM, length), lambda g, s: (3 * groups + g, 0)),
    ]


def attend(side, qkv, doc_q, doc_k):
    hidden, length = qkv.shape
    groups = hidden // (4 * HEAD_DIM)
    whole = lambda g, s: (0, 0)
    spec = pl.BlockSpec
    return pl.pallas_call(
        forward_kernel,
        grid_spec=pltpu.PrefetchScalarGridSpec(
            num_scalar_prefetch=1,
            grid=(groups,),
            in_specs=group_specs(groups, length) + [spec((DOCS, length), whole)] * 2,
            out_specs=[
                spec((2 * HEAD_DIM, length), lambda g, s: (g, 0)),
                spec((1, 2, length), lambda g, s: (g, 0, 0)),
            ],
            scratch_shapes=[
                pltpu.VMEM((PAD_DIM, length), BF16),
                pltpu.VMEM((PAD_DIM, length), BF16),
                pltpu.VMEM((length, PAD_DIM), BF16),
                pltpu.VMEM((PAD_DIM, length), BF16),
            ],
        ),
        out_shape=[
            jax.ShapeDtypeStruct((2 * groups * HEAD_DIM, length), BF16),
            jax.ShapeDtypeStruct((groups, 2, length), F32),
        ],
        compiler_params=pltpu.CompilerParams(vmem_limit_bytes=VMEM),
        cost_estimate=FREE,
        name="attend",
    )(side, qkv, qkv, qkv, doc_q, doc_k)


def backward_kernel(
    side_ref, q_ref, k_ref, v_ref, att_ref, datt_own, datt_par, lse_ref, cos_ref, sin_ref,
    oq_ref, ok_ref, *rest,
):
    out_ref, *rest = rest
    q_scr, kt_scr, k_scr, vt_scr, v_scr, do_scr, dk_scr, dv_scr, datt_ref, dq_ref, sem = rest
    length = q_ref.shape[1]
    group = pl.program_id(0)
    groups = out_ref.shape[0] // (4 * HEAD_DIM)
    datt_ref[:, : length // 2] = datt_own[...]
    datt_ref[:, length // 2 :] = datt_par[...]
    slot = lax.rem(group, 2)
    dk_ref = dq_ref.at[slot, 2 * HEAD_DIM : 3 * HEAD_DIM, :]
    dv_ref = dq_ref.at[slot, 3 * HEAD_DIM :, :]
    dq_ref = dq_ref.at[slot]

    def stores(number, source):
        for i, (start, size) in enumerate(((0, 2), (2, 1), (3, 1))):
            base = (start * groups + number * size) * HEAD_DIM
            yield pltpu.make_async_copy(
                rest[-2].at[source, start * HEAD_DIM : (start + size) * HEAD_DIM, :],
                out_ref.at[pl.ds(pl.multiple_of(base, HEAD_DIM), size * HEAD_DIM), :],
                sem.at[source, i],
            )

    half = HEAD_DIM // 2
    side = side_ref[0]
    blocks = length // BLOCK
    fill(kt_scr, k_ref, side, ok_ref)
    fill(vt_scr, v_ref, side, None)
    k_scr[...] = kt_scr[...].T
    v_scr[...] = vt_scr[...].T
    causal = diagonal()
    for h in range(2):
        rows = slice(h * HEAD_DIM, (h + 1) * HEAD_DIM)
        fill(q_scr, q_ref.at[rows, :], side, oq_ref)
        fill(do_scr, datt_ref.at[rows, :], side, None)
        for b in range(blocks):
            here = pl.ds(b * BLOCK, BLOCK)
            there = pl.ds(place_of(b * BLOCK, side, length), BLOCK)
            base = jnp.sum(
                datt_ref[rows, there].astype(F32) * att_ref[rows, there].astype(F32), 0, keepdims=True
            )
            keys = (b + 1) * BLOCK
            query, upstream = q_scr[:, here], do_scr[:, here]
            level = lse_ref[0, h : h + 1, here]
            dq = None
            for start, stop in ((b * BLOCK, keys), (0, b * BLOCK)):
                if start == stop:
                    continue
                span = slice(start, stop)
                score = mm(k_scr[span, :], query, 1, 0)
                prob = jnp.exp2(score * (SCALE * LOG2E) - level)
                if stop == keys:
                    prob = jnp.where(causal, prob, 0.0)
                slope = mm(v_scr[span, :], upstream, 1, 0)
                ds = (prob * (slope - base)).astype(BF16)
                part = mm(kt_scr[:HEAD_DIM, span], ds, 1, 0)
                dq = part if dq is None else dq + part
                dk = mm(query[:HEAD_DIM, :], ds, 1, 1)
                dv = mm(upstream[:HEAD_DIM, :], prob.astype(BF16), 1, 1)
                if h == 0 and stop == keys:
                    dk_scr[:, span] = dk
                    dv_scr[:, span] = dv
                else:
                    dk_scr[:, span] += dk
                    dv_scr[:, span] += dv
            cos, sin = cos_ref[:, there], sin_ref[:, there]
            dq = dq * SCALE
            top, bottom = rope_rows(dq[:half, :], dq[half:, :], cos, -sin)
            dq_ref[h * HEAD_DIM : h * HEAD_DIM + half, there] = top.astype(BF16)
            dq_ref[h * HEAD_DIM + half : (h + 1) * HEAD_DIM, there] = bottom.astype(BF16)
    for b in range(blocks):
        here = pl.ds(b * BLOCK, BLOCK)
        there = pl.ds(place_of(b * BLOCK, side, length), BLOCK)
        cos, sin = cos_ref[:, there], sin_ref[:, there]
        dk = dk_scr[:, here] * SCALE
        top, bottom = rope_rows(dk[:half, :], dk[half:, :], cos, -sin)
        dk_ref[:half, there] = top.astype(BF16)
        dk_ref[half:, there] = bottom.astype(BF16)
        dv_ref[:, there] = dv_scr[:, here].astype(BF16)
    for copy in stores(group, slot):
        copy.start()

    @pl.when(group > 0)
    def _():
        for copy in stores(group - 1, 1 - slot):
            copy.wait()

    @pl.when(group == pl.num_programs(0) - 1)
    def _():
        for copy in stores(group, slot):
            copy.wait()


def attend_back(side, qkv, att, datt, lse, cos, sin, doc_q, doc_k):
    hidden, length = qkv.shape
    groups = hidden // (4 * HEAD_DIM)
    whole = lambda g, s: (0, 0)
    spec = pl.BlockSpec
    narrow = spec((2 * HEAD_DIM, length // 2), lambda g, s: (g, 0))
    source = spec((2 * HEAD_DIM, length), lambda g, s: (g, 0))
    level = spec((1, 2, length), lambda g, s: (g, 0, 0))
    anywhere = spec(memory_space=pl.ANY)
    table = spec((HEAD_DIM // 2, length), whole)
    docs = spec((DOCS, length), whole)
    tall = pltpu.VMEM((length, PAD_DIM), BF16)
    flat = pltpu.VMEM((PAD_DIM, length), BF16)
    return pl.pallas_call(
        backward_kernel,
        grid_spec=pltpu.PrefetchScalarGridSpec(
            num_scalar_prefetch=1,
            grid=(groups,),
            in_specs=group_specs(groups, length)
            + [source, narrow, narrow, level, table, table, docs, docs],
            out_specs=anywhere,
            scratch_shapes=[flat, flat, tall, flat, tall, flat]
            + [pltpu.VMEM((HEAD_DIM, length), F32)] * 2
            + [
                pltpu.VMEM((2 * HEAD_DIM, length), BF16),
                pltpu.VMEM((2, 4 * HEAD_DIM, length), BF16),
                pltpu.SemaphoreType.DMA((2, 3)),
            ],
        ),
        out_shape=jax.ShapeDtypeStruct((hidden, length), BF16),
        compiler_params=pltpu.CompilerParams(vmem_limit_bytes=VMEM),
        cost_estimate=FREE,
        name="attend_back",
    )(side, qkv, qkv, qkv, att, *datt, lse, cos, sin, doc_q, doc_k)


def low(weight):
    return weight.astype(BF16)


def layer(
    dp, tokens, segment_ids, positions, query_weight, key_weight, value_weight, out_weight,
    attn_gain, gate_weight, up_weight, down_weight, mlp_gain, cotangent,
):
    seqs, own_rows, model = tokens.shape
    length = segment_ids.shape[1]
    heads = query_weight.shape[1]
    ff = gate_weight.shape[1]
    side_index = lax.axis_index("tensor").astype(jnp.int32)
    side = side_index[None]
    blocks, turned = piece_blocks(dp), turn_blocks(dp)

    x_own = tokens.reshape(own_rows, model)
    e_own = cotangent.reshape(own_rows, model)
    gains = jnp.pad(jnp.stack([low(attn_gain), low(mlp_gain)], 1), ((0, 0), (0, 126)))
    order = Order(positions[0, 0] >= 0)
    first = order.done(join(query_weight, key_weight, value_weight, out_weight.T, gains))
    first = Gather(first, dp, 1280)
    x_par = swap_halves(x_own)
    first.round(order)
    first.share(order)
    second = order.done(join(gate_weight, up_weight, down_weight.T))
    second = Gather(second, dp, 3 * ff // 2)
    for _ in range(dp // 4 - 1):
        first.next(order)
    second.share(order)
    first = first.pieces(order)
    x_first, x_par = order.done(*order.tie(x_own, x_par))
    e_par = swap_halves(order.tie(e_own))
    second.round(order)

    places = positions.reshape(length).astype(F32)
    half = HEAD_DIM // 2
    places = jnp.where(side_index == 0, places, jnp.roll(places, length // 2))
    ladder = jnp.power(F32(ROPE_BASE), -2.0 * jnp.arange(half, dtype=F32) / HEAD_DIM)
    angles = ladder[:, None] * places[None, :]
    cos, sin = jnp.cos(angles), jnp.sin(angles)
    known = jnp.arange(DOCS, dtype=jnp.int32)[:, None] == segment_ids.reshape(1, length)
    doc_q = known.astype(BF16)
    doc_k = jnp.where(known, 0.0, -FAR).astype(BF16)

    qkv, gain_rows, a_turned, qkv_full, out_full = project(
        blocks, turned, x_first, x_par, cos, sin, first, heads
    )
    qkv = order.done(qkv)
    att, lse = attend(side, order.tie(qkv), doc_q, doc_k)
    e_par, att = order.done(e_par, att)

    own, par = slice(0, own_rows), slice(own_rows, None)
    partial = order.done(mm(att[:, par], out_full, 0, 1, BF16))
    sent = swap_halves(partial)
    second.next(order)
    e_turned = order.done(turn(turned, order.tie(e_own), e_par))
    partial = order.done(mm(att[:, own], order.tie(out_full), 0, 1))
    second.next(order)
    sent = order.tie(sent)
    middle, b_own = order.done(
        *by_rows(residual_kernel, (partial, sent, x_own), gain_rows, (F32, BF16), "residual")
    )
    b_par = swap_halves(b_own)
    second.next(order)
    second = second.pieces(order)

    b_par = order.tie(b_par)
    hidden, pair, db_own, db_par, down_full = ffn(blocks, b_own, b_par, e_own, e_par, second)
    db_par = order.done(db_par)
    db_sent = swap_halves(db_par)
    b_turned = order.done(turn(turned, order.tie(b_own), b_par))
    grad_ffn = Scatter(dp, order, (e_turned, hidden, 0), (b_turned, pair, 0))
    dh, eh_own = order.done(
        *by_rows(
            functools.partial(back_kernel, 1),
            (db_own, order.tie(db_sent), middle, e_own),
            gain_rows,
            (F32, BF16),
            "norm_back",
        )
    )
    eh_par = swap_halves(eh_own)
    grad_ffn.round()
    down_own, down_par = order.done(*product(order.tie(hidden), down_full))
    grad_ffn.round()
    datt_own = order.done(turned_product(order.tie(eh_own), out_full, 384))
    eh_par = order.tie(eh_par)
    datt_par = order.done(turned_product(eh_par, out_full, 384))
    down_sent = swap_halves(order.tie(down_par))
    eh_turned = order.done(turn(turned, order.tie(eh_own), eh_par))
    grad_ffn.round()
    datt = order.tie(datt_own, datt_par)
    dqkv = order.done(attend_back(side, qkv, att, datt, lse, cos, sin, doc_q, doc_k))
    down_sent = order.done(down_sent)
    da = order.done(turned_product(qkv_full, order.tie(dqkv), own_rows))
    da_sent = swap_halves(da[par])
    grad_ffn.round()
    grad_att = Scatter(dp, order, (a_turned, dqkv, 1), (eh_turned, att, 1))
    grad_att.round()
    output = (middle + (down_own.astype(F32) + order.tie(down_sent).astype(F32))).astype(BF16)
    output = order.done(output)
    grad_gate, grad_up, grad_down, gain_two = grad_ffn.result(
        (
            (ff, TILE, 2 * TILE, ff // TILE),
            (ff + TILE, TILE, 2 * TILE, ff // TILE),
            (0, TILE, TILE, ff // TILE),
        ),
        (gate_weight, up_weight),
    )
    grad_att.round()
    da_sent = order.done(da_sent)
    grad_att.round()
    (input_grad,) = by_rows(
        functools.partial(back_kernel, 0),
        (order.tie(da[own]), da_sent, x_own, dh),
        gain_rows,
        (BF16,),
        "norm_back",
    )
    input_grad = order.done(input_grad)
    grad_att.round()
    kv = heads // 2
    size = kv // 3 if kv % 384 else 384
    grad_query, grad_key, grad_value, grad_out, gain_one = grad_att.result(
        (
            (0, size, size, heads // size),
            (heads, size, size, kv // size),
            (heads + kv, size, size, kv // size),
            (2 * heads, size, size, heads // size),
        ),
        (query_weight, key_weight, value_weight),
    )
    gain_grads = jnp.stack(
        [gain_one[0] / low(attn_gain).astype(F32), gain_two[0] / low(mlp_gain).astype(F32)]
    )
    gain_grads = gain_grads + swap_halves(gain_grads)
    return (
        output.reshape(seqs, own_rows, model),
        input_grad.reshape(seqs, own_rows, model),
        grad_query,
        grad_key,
        grad_value,
        grad_out.T,
        gain_grads[0],
        grad_gate,
        grad_up,
        grad_down.T,
        gain_grads[1],
    )


def solution(mesh):
    in_specs = (
        P("dp", "tensor", None),
        P("dp", None),
        P("dp", None),
        P("dp", "tensor"),
        P("dp", "tensor"),
        P("dp", "tensor"),
        P("tensor", "dp"),
        P("dp"),
        P("dp", "tensor"),
        P("dp", "tensor"),
        P("tensor", "dp"),
        P("dp"),
        P("dp", "tensor", None),
    )
    out_specs = (
        P("dp", "tensor", None),
        P("dp", "tensor", None),
        P("dp", "tensor"),
        P("dp", "tensor"),
        P("dp", "tensor"),
        P("tensor", "dp"),
        P("dp"),
        P("dp", "tensor"),
        P("dp", "tensor"),
        P("tensor", "dp"),
        P("dp"),
    )
    return jax.shard_map(
        functools.partial(layer, mesh.shape["dp"]),
        mesh=mesh,
        in_specs=in_specs,
        out_specs=out_specs,
        check_vma=False,
    )
```

profile of v0, /device:TPU:0, one launch (start us, length us, event | category | flops | bytes accessed | tf_op | source)
XLA Modules:
  0.0 463.1 jit_solution(9322096720419668025)
XLA Ops:
  24.4 6.7 %collective-permute-done.22.rest_2_ = bf16[96,2432]{1,0:T(8,128)(2,1)} collective-permute-done((bf16[96,2432]{1,0:T(8,128)(2,1)}, bf16[96,2432]{1,0:T(8,128)(2,1)}, u32[]{:S(2)}, u32[]{:S(2)}) %collective-permute-start.22) | collective-permute-done | bytes 466976 | tf_op jit(solution)/shard_map/ppermute | solution.py:131
  37.4 5.3 %collective-permute-done.24.left_ref.rest_3_ = bf16[96,2432]{1,0:T(8,128)(2,1)S(1)} collective-permute-done((bf16[96,2432]{1,0:T(8,128)(2,1)}, bf16[96,2432]{1,0:T(8,128)(2,1)S(1)}, u32[]{:S(2)}, u32[]{:S(2)}) %collective-permute-start.24) | collective-permute-done | bytes 466976 | tf_op jit(solution)/shard_map/ppermute | solution.py:131
  63.2 18.0 %project.1 = (bf16[1536,1024]{1,0:T(8,128)(2,1)}, f32[8,1536]{1,0:T(8,128)}, bf16[1536,1024]{1,0:T(8,128)(2,1)}, bf16[1536,1536]{1,0:T(8,128)(2,1)}, bf16[1536,768]{1,0:T(8,128)(2,1)}) custom-call(s32[18]{0:T(128)} %pad_add_fusion.block_ref, s32[16]{0:T(128)} %pad_add_fusion.1.turn_ref, bf16[512,1536]{1,0:T(8,128)(2,1)} %bitcast.35, ...), custom_call_target="tpu_custom_call" | custom-call | tf_op jit(solution)/shard_map/project/pallas_call | solution.py:626
  81.2 14.9 %attend.1 = (bf16[768,1024]{1,0:T(8,128)(2,1)}, f32[4,2,1024]{2,1,0:T(2,128)}) custom-call(s32[1]{0:T(128)} %bitcast.8.side_ref, bf16[1536,1024]{1,0:T(8,128)(2,1)} %get-tuple-element.611.q_in.k_in.v_in.q_ref.k_ref.v_ref, bf16[1536,1024]{1,0:T(8,128)(2,1)} %get-tuple-element.611.q_in.k_in.v_in.q_ref.k_ref.v_ref, ...), custom_call_target="tpu_custom_call" | custom-call | tf_op jit(solution)/shard_map/attend/pallas_call | solution.py:866
  103.1 5.1 %conditional.18 = (bf16[96,6144]{1,0:T(8,128)(2,1)}, bf16[96,6144]{1,0:T(8,128)(2,1)}) conditional(s32[]{:T(128)} %bitcast.3, () %tuple.245, (bf16[96,6144]{1,0:T(8,128)(2,1)}, bf16[96,6144]{1,0:T(8,128)(2,1)}) %tuple.247), branch_computations={%region_12.13_spmd, %region_13.14_spmd} | conditional | bytes 9437280 | solution.py:118
  108.1 6.0 %turn.3 = bf16[1536,1024]{1,0:T(8,128)(2,1)} custom-call(s32[16]{0:T(128)} %pad_add_fusion.1.turn_ref, bf16[512,1536]{1,0:T(8,128)(2,1)} %bitcast.7.own_ref.e_own.base_ref, bf16[512,1536]{1,0:T(8,128)(2,1)} %collective-permute-done.29.par_ref.e_par), custom_call_target="tpu_custom_call" | custom-call | bytes 41943040 | tf_op jit(solution)/shard_map/turn/pallas_call | solution.py:598
  114.1 5.0 %fusion.part_ref = f32[512,1536]{1,0:T(8,128)} fusion(bf16[1536,768]{1,0:T(8,128)(2,1)} %get-tuple-element.503.right_ref, bf16[768,1024]{1,0:T(8,128)(2,1)} %get-tuple-element.634.att_ref), kind=kOutput, calls=%fused_computation.2 | convolution fusion | flops 1207959552 | bytes 6291456 | tf_op jit(solution)/shard_map/dot_general | solution.py:29
  119.1 9.2 %collective-permute-done.32.rest_2_ = bf16[96,6144]{1,0:T(8,128)(2,1)} collective-permute-done((bf16[96,6144]{1,0:T(8,128)(2,1)}, bf16[96,6144]{1,0:T(8,128)(2,1)}, u32[]{:S(2)}, u32[]{:S(2)}) %collective-permute-start.32) | collective-permute-done | bytes 1179680 | tf_op jit(solution)/shard_map/ppermute | solution.py:131
  131.5 4.9 %conditional.19 = (bf16[96,6144]{1,0:T(8,128)(2,1)}, bf16[96,6144]{1,0:T(8,128)(2,1)}) conditional(s32[]{:T(128)} %bitcast.3, () %tuple.255, (bf16[96,6144]{1,0:T(8,128)(2,1)}, bf16[96,6144]{1,0:T(8,128)(2,1)}) %tuple.257), branch_computations={%region_14.15_spmd, %region_15.16_spmd} | conditional | bytes 9437280 | solution.py:118
  136.5 5.5 %residual.1 = (f32[512,1536]{1,0:T(8,128)}, bf16[512,1536]{1,0:T(8,128)(2,1)}) custom-call(f32[512,1536]{1,0:T(8,128)} %fusion.part_ref, bf16[512,1536]{1,0:T(8,128)(2,1)} %collective-permute-done.34.sent_ref, bf16[512,1536]{1,0:T(8,128)(2,1)} %bitcast.36, f32[8,1536]{1,0:T(8,128)} %get-tuple-element.521.gain_ref), custom_call_target="tpu_custom_call" | custom-call | tf_op jit(solution)/shard_map/residual/pallas_call | solution.py:480
  143.5 12.0 %collective-permute-done.35.left_ref.rest_3_ = bf16[96,6144]{1,0:T(8,128)(2,1)} collective-permute-done((bf16[96,6144]{1,0:T(8,128)(2,1)}, bf16[96,6144]{1,0:T(8,128)(2,1)}, u32[]{:S(2)}, u32[]{:S(2)}) %collective-permute-start.35) | collective-permute-done | bytes 1179680 | tf_op jit(solution)/shard_map/ppermute | solution.py:131
  165.6 5.2 %collective-permute-done.37.rest_7_ = bf16[96,3072]{1,0:T(8,128)(2,1)S(1)} collective-permute-done((bf16[96,3072]{1,0:T(8,128)(2,1)}, bf16[96,3072]{1,0:T(8,128)(2,1)S(1)}, u32[]{:S(2)}, u32[]{:S(2)}) %collective-permute-start.37) | collective-permute-done | bytes 589856 | tf_op jit(solution)/shard_map/ppermute | solution.py:131
  178.7 45.9 %ffn.1 = (bf16[1024,2048]{1,0:T(8,128)(2,1)}, bf16[1024,4096]{1,0:T(8,128)(2,1)}, f32[512,1536]{1,0:T(8,128)}, bf16[512,1536]{1,0:T(8,128)(2,1)}, bf16[1536,2048]{1,0:T(8,128)(2,1)}) custom-call(s32[18]{0:T(128)} %pad_add_fusion.block_ref, bf16[512,1536]{1,0:T(8,128)(2,1)} %get-tuple-element.563.b_own.own_ref, ...), custom_call_target="tpu_custom_call" | custom-call | tf_op jit(solution)/shard_map/ffn/pallas_call | solution.py:758
  226.2 6.1 %turn.4 = bf16[1536,1024]{1,0:T(8,128)(2,1)} custom-call(s32[16]{0:T(128)} %pad_add_fusion.1.turn_ref, bf16[512,1536]{1,0:T(8,128)(2,1)} %get-tuple-element.563.b_own.own_ref, bf16[512,1536]{1,0:T(8,128)(2,1)} %collective-permute-done.39.b_par.par_ref), custom_call_target="tpu_custom_call" | custom-call | bytes 41943040 | tf_op jit(solution)/shard_map/turn/pallas_call | solution.py:598
  232.3 33.8 %conditional.22 = (bf16[768,6144]{1,0:T(8,128)(2,1)}, bf16[768,6144]{1,0:T(8,128)(2,1)}) conditional(s32[]{:T(128)} %bitcast.3, () %tuple.275, (bf16[1536,1024]{1,0:T(8,128)(2,1)}, bf16[1536,1024]{1,0:T(8,128)(2,1)}, bf16[1024,2048]{1,0:T(8,128)(2,1)}, bf16[1024,4096]{1,0:T(8,128)(2,1)}) %tuple.277), branch_computations={%region_20.21_spmd, %region_21.22_spmd} | conditional | bytes 37748792 | solution.py:187
  232.7 16.7 %products.4 = bf16[768,6144]{1,0:T(8,128)(2,1)} custom-call(bf16[1536,1024]{1,0:T(8,128)(2,1)} %get-tuple-element.72.refs_0_, bf16[1536,1024]{1,0:T(8,128)(2,1)} %get-tuple-element.73.refs_1_, bf16[1024,2048]{1,0:T(8,128)(2,1)} %get-tuple-element.78.refs_2_, bf16[1024,4096]{1,0:T(8,128)(2,1)} %get-tuple-element.79.refs_3_), custom_call_target="tpu_custom_call" | custom-call | tf_op jit(solution)/shard_map/cond/branch_1_fun/products/pallas_call | solution.py:385
  249.4 16.7 %products.5 = bf16[768,6144]{1,0:T(8,128)(2,1)} custom-call(bf16[1536,1024]{1,0:T(8,128)(2,1)} %get-tuple-element.72.refs_0_, bf16[1536,1024]{1,0:T(8,128)(2,1)} %get-tuple-element.73.refs_1_, bf16[1024,2048]{1,0:T(8,128)(2,1)} %get-tuple-element.78.refs_2_, bf16[1024,4096]{1,0:T(8,128)(2,1)} %get-tuple-element.79.refs_3_), custom_call_target="tpu_custom_call" | custom-call | tf_op jit(solution)/shard_map/cond/branch_1_fun/products/pallas_call | solution.py:385
  266.1 6.9 %norm_back.2 = (f32[512,1536]{1,0:T(8,128)}, bf16[512,1536]{1,0:T(8,128)(2,1)}) custom-call(f32[512,1536]{1,0:T(8,128)} %get-tuple-element.574.own_ref, bf16[512,1536]{1,0:T(8,128)(2,1)} %collective-permute-done.40.sent_ref, f32[512,1536]{1,0:T(8,128)} %get-tuple-element.577.value_ref, bf16[512,1536]{1,0:T(8,128)(2,1)} %bitcast.7.own_ref.e_own.base_ref, ...), custom_call_target="tpu_custom_call" | custom-call | tf_op jit(solution)/shard_map/norm_back/pallas_call | solution.py:480
  278.0 11.9 %product.1 = (bf16[512,1536]{1,0:T(8,128)(2,1)}, bf16[512,1536]{1,0:T(8,128)(2,1)}) custom-call(bf16[1024,2048]{1,0:T(8,128)(2,1)} %get-tuple-element.587.left_ref, bf16[1536,2048]{1,0:T(8,128)(2,1)} %get-tuple-element.588.right_ref), custom_call_target="tpu_custom_call" | custom-call | tf_op jit(solution)/shard_map/product/pallas_call | solution.py:336
  303.9 6.2 %collective-permute-done.43.left_ref.par_ref = bf16[512,1536]{1,0:T(8,128)(2,1)} collective-permute-done((bf16[512,1536]{1,0:T(8,128)(2,1)}, bf16[512,1536]{1,0:T(8,128)(2,1)}, u32[]{:S(2)}, u32[]{:S(2)}) %collective-permute-start.43) | collective-permute-done | bytes 1572896 | tf_op jit(solution)/shard_map/ppermute | solution.py:35
  315.3 6.0 %turn.5 = bf16[1536,1024]{1,0:T(8,128)(2,1)} custom-call(s32[16]{0:T(128)} %pad_add_fusion.1.turn_ref, bf16[512,1536]{1,0:T(8,128)(2,1)} %get-tuple-element.603.left_ref.own_ref, bf16[512,1536]{1,0:T(8,128)(2,1)} %collective-permute-done.43.left_ref.par_ref), custom_call_target="tpu_custom_call" | custom-call | bytes 41943040 | tf_op jit(solution)/shard_map/turn/pallas_call | solution.py:598
  325.4 5.1 %combine.10 = (bf16[96,6144]{1,0:T(8,128)(2,1)}, bf16[96,6144]{1,0:T(8,128)(2,1)}) custom-call(bf16[768,6144]{1,0:T(8,128)(2,1)} %get-tuple-element.649.refs_0_.refs_2_.refs_3_, bf16[768,6144]{1,0:T(8,128)(2,1)} %get-tuple-element.583.refs_1_.refs_3_.refs_4_, bf16[96,6144]{1,0:T(8,128)(2,1)} %collective-permute-done.44.refs_2_, ...), custom_call_target="tpu_custom_call" | custom-call | tf_op jit(solution)/shard_map/combine/pallas_call | solution.py:560
  332.7 21.9 %attend_back.1.right_ref = bf16[1536,1024]{1,0:T(8,128)(2,1)} custom-call(s32[1]{0:T(128)} %bitcast.8.side_ref, bf16[1536,1024]{1,0:T(8,128)(2,1)} %get-tuple-element.611.q_in.k_in.v_in.q_ref.k_ref.v_ref, bf16[1536,1024]{1,0:T(8,128)(2,1)} %get-tuple-element.611.q_in.k_in.v_in.q_ref.k_ref.v_ref, ...), custom_call_target="tpu_custom_call" | custom-call | tf_op jit(solution)/shard_map/attend_back/pallas_call | solution.py:1001
  354.6 9.4 %turned_product.5 = bf16[1024,1536]{1,0:T(8,128)(2,1)} custom-call(bf16[1536,1536]{1,0:T(8,128)(2,1)} %get-tuple-element.621.left_ref, bf16[1536,1024]{1,0:T(8,128)(2,1)} %attend_back.1.right_ref), custom_call_target="tpu_custom_call" | custom-call | tf_op jit(solution)/shard_map/turned_product/pallas_call | solution.py:405
  364.1 5.1 %combine.11 = (bf16[96,6144]{1,0:T(8,128)(2,1)}, bf16[96,6144]{1,0:T(8,128)(2,1)}) custom-call(bf16[768,6144]{1,0:T(8,128)(2,1)} %get-tuple-element.649.refs_0_.refs_2_.refs_3_, bf16[768,6144]{1,0:T(8,128)(2,1)} %get-tuple-element.583.refs_1_.refs_3_.refs_4_, bf16[96,6144]{1,0:T(8,128)(2,1)} %collective-permute-done.47.refs_2_, ...), custom_call_target="tpu_custom_call" | custom-call | tf_op jit(solution)/shard_map/combine/pallas_call | solution.py:560
  376.4 16.6 %conditional.23 = (bf16[768,2304]{1,0:T(8,128)(2,1)}, bf16[768,2304]{1,0:T(8,128)(2,1)}) conditional(s32[]{:T(128)} %bitcast.3, () %tuple.303, (bf16[1536,1024]{1,0:T(8,128)(2,1)}, bf16[1536,1024]{1,0:T(8,128)(2,1)}, bf16[1536,1024]{1,0:T(8,128)(2,1)}, bf16[768,1024]{1,0:T(8,128)(2,1)}) %tuple.305), branch_computations={%region_22.23_spmd, %region_23.24_spmd} | conditional | bytes 14155832 | solution.py:187
  376.4 8.3 %products.6 = bf16[768,2304]{1,0:T(8,128)(2,1)} custom-call(bf16[1536,1024]{1,0:T(8,128)(2,1)} %get-tuple-element.80.refs_0_, bf16[1536,1024]{1,0:T(8,128)(2,1)} %get-tuple-element.81.refs_1_, bf16[1536,1024]{1,0:T(8,128)(2,1)} %get-tuple-element.86.refs_2_, bf16[768,1024]{1,0:T(8,128)(2,1)} %get-tuple-element.87.refs_3_), custom_call_target="tpu_custom_call" | custom-call | tf_op jit(solution)/shard_map/cond/branch_1_fun/products/pallas_call | solution.py:385
  384.7 8.3 %products.7 = bf16[768,2304]{1,0:T(8,128)(2,1)} custom-call(bf16[1536,1024]{1,0:T(8,128)(2,1)} %get-tuple-element.80.refs_0_, bf16[1536,1024]{1,0:T(8,128)(2,1)} %get-tuple-element.81.refs_1_, bf16[1536,1024]{1,0:T(8,128)(2,1)} %get-tuple-element.86.refs_2_, bf16[768,1024]{1,0:T(8,128)(2,1)} %get-tuple-element.87.refs_3_), custom_call_target="tpu_custom_call" | custom-call | tf_op jit(solution)/shard_map/cond/branch_1_fun/products/pallas_call | solution.py:385
  402.0 5.1 %finish.2 = (f32[96,2048]{1,0:T(8,128)}, f32[96,2048]{1,0:T(8,128)}, f32[96,2048]{1,0:T(8,128)}, f32[8,96]{1,0:T(8,128)}) custom-call(bf16[768,6144]{1,0:T(8,128)(2,1)} %get-tuple-element.649.refs_0_.refs_2_.refs_3_, bf16[768,6144]{1,0:T(8,128)(2,1)} %get-tuple-element.583.refs_1_.refs_3_.refs_4_, bf16[96,6144]{1,0:T(8,128)(2,1)} %collective-permute-done.49.refs_2_, ...), custom_call_target="tpu_custom_call" | custom-call | tf_op jit(solution)/shard_map/finish/pallas_call | solution.py:520
  413.1 10.2 %collective-permute-done.54.refs_2_ = bf16[96,2304]{1,0:T(8,128)(2,1)S(1)} collective-permute-done((bf16[96,2304]{1,0:T(8,128)(2,1)}, bf16[96,2304]{1,0:T(8,128)(2,1)S(1)}, u32[]{:S(2)}, u32[]{:S(2)}) %collective-permute-start.54) | collective-permute-done | bytes 442400 | tf_op jit(solution)/shard_map/ppermute | solution.py:213
  429.6 5.6 %norm_back.3 = bf16[512,1536]{1,0:T(8,128)(2,1)} custom-call(bf16[512,1536]{1,0:T(8,128)(2,1)} %get-tuple-element.671.own_ref, bf16[512,1536]{1,0:T(8,128)(2,1)} %collective-permute-done.53.sent_ref, bf16[512,1536]{1,0:T(8,128)(2,1)} %bitcast.37, f32[512,1536]{1,0:T(8,128)} %get-tuple-element.673.base_ref, f32[8,1536]{1,0:T(8,128)} %get-tuple-element.521.gain_ref), custom_call_target="tpu_custom_call" | custom-call | tf_op jit(solution)/shard_map/norm_back/pallas_call | solution.py:480
  445.9 7.7 %collective-permute-done.58.refs_2_ = bf16[96,2304]{1,0:T(8,128)(2,1)S(1)} collective-permute-done((bf16[96,2304]{1,0:T(8,128)(2,1)}, bf16[96,2304]{1,0:T(8,128)(2,1)S(1)}, u32[]{:S(2)}, u32[]{:S(2)}) %collective-permute-start.58) | collective-permute-done | bytes 442400 | tf_op jit(solution)/shard_map/ppermute | solution.py:213
  (190 shorter events, 194.1 us)
Async XLA Ops:
  4.1 13.9 %collective-permute-start.20 = (bf16[96,2432]{1,0:T(8,128)(2,1)}, bf16[96,2432]{1,0:T(8,128)(2,1)}, u32[]{:S(2)}, u32[]{:S(2)}) collective-permute-start(bf16[96,2432]{1,0:T(8,128)(2,1)} %join.2.rest_0_), channel_id=1, source_target_pairs={{0,8},{2,10},{8,16},{10,18},{16,24},{18,26},{24,28},{26,30},{28,20... | collective-permute-start | bytes 1400840 | tf_op jit(solution)/shard_map/ppermute | solution.py:131
  7.1 12.5 %collective-permute-start.21 = (bf16[96,2432]{1,0:T(8,128)(2,1)}, bf16[96,2432]{1,0:T(8,128)(2,1)}, u32[]{:S(2)}, u32[]{:S(2)}) collective-permute-start(bf16[96,2432]{1,0:T(8,128)(2,1)} %join.2.rest_0_), channel_id=1, source_target_pairs={{8,0},{10,2},{16,8},{18,10},{24,16},{26,18},{28,24},{30,26},{20,28... | collective-permute-start | bytes 1400840 | tf_op jit(solution)/shard_map/ppermute | solution.py:132
  7.1 48.6 %collective-permute-start.28 = (bf16[512,1536]{1,0:T(8,128)(2,1)}, bf16[512,1536]{1,0:T(8,128)(2,1)}, u32[]{:S(2)}, u32[]{:S(2)}) collective-permute-start(bf16[512,1536]{1,0:T(8,128)(2,1)} %bitcast.34), channel_id=1, source_target_pairs={{0,1},{1,0},{2,3},{3,2},{4,5},{5,4},{6,7},{7,6},{8,9},{9,8},{10,11... | collective-permute-start | bytes 4718600 | tf_op jit(solution)/shard_map/ppermute | solution.py:35
  19.6 11.6 %collective-permute-start.22 = (bf16[96,2432]{1,0:T(8,128)(2,1)}, bf16[96,2432]{1,0:T(8,128)(2,1)}, u32[]{:S(2)}, u32[]{:S(2)}) collective-permute-start(bf16[96,2432]{1,0:T(8,128)(2,1)} %collective-permute-done.20.rest_1_), channel_id=1, source_target_pairs={{0,8},{2,10},{8,16},{10,18},{16,24},{18,26},{24,28},{26,30},{28,20... | collective-permute-start | bytes 1400840 | tf_op jit(solution)/shard_map/ppermute | solution.py:131
  55.7 40.4 %collective-permute-start.29 = (bf16[512,1536]{1,0:T(8,128)(2,1)}, bf16[512,1536]{1,0:T(8,128)(2,1)}, u32[]{:S(2)}, u32[]{:S(2)}) collective-permute-start(bf16[512,1536]{1,0:T(8,128)(2,1)} %bitcast.7.own_ref.e_own.base_ref), channel_id=1, source_target_pairs={{0,1},{1,0},{2,3},{3,2},{4,5},{5,4},{6,7},{7,6},{8,9},{9,8},{10,11... | collective-permute-start | bytes 4718600 | tf_op jit(solution)/shard_map/ppermute | solution.py:35
  57.9 43.2 %collective-permute-start.30 = (bf16[96,6144]{1,0:T(8,128)(2,1)}, bf16[96,6144]{1,0:T(8,128)(2,1)}, u32[]{:S(2)}, u32[]{:S(2)}) collective-permute-start(bf16[96,6144]{1,0:T(8,128)(2,1)} %join.3.rest_0_), channel_id=1, source_target_pairs={{0,8},{2,10},{8,16},{10,18},{16,24},{18,26},{24,28},{26,30},{28,20... | collective-permute-start | bytes 3538952 | tf_op jit(solution)/shard_map/ppermute | solution.py:131
  59.3 41.7 %collective-permute-start.31 = (bf16[96,6144]{1,0:T(8,128)(2,1)}, bf16[96,6144]{1,0:T(8,128)(2,1)}, u32[]{:S(2)}, u32[]{:S(2)}) collective-permute-start(bf16[96,6144]{1,0:T(8,128)(2,1)} %join.3.rest_0_), channel_id=1, source_target_pairs={{8,0},{10,2},{16,8},{18,10},{24,16},{26,18},{28,24},{30,26},{20,28... | collective-permute-start | bytes 3538952 | tf_op jit(solution)/shard_map/ppermute | solution.py:132
  100.6 35.9 %collective-permute-start.34 = (bf16[512,1536]{1,0:T(8,128)(2,1)}, bf16[512,1536]{1,0:T(8,128)(2,1)}, u32[]{:S(2)}, u32[]{:S(2)}) collective-permute-start(bf16[512,1536]{1,0:T(8,128)(2,1)} %convolution_convert_fusion), channel_id=1, source_target_pairs={{0,1},{1,0},{2,3},{3,2},{4,5},{5,4},{6,7},{7,6},{8,9},{9,8},{10,11... | collective-permute-start | bytes 4718600 | tf_op jit(solution)/shard_map/ppermute | solution.py:35
  101.0 27.2 %collective-permute-start.32 = (bf16[96,6144]{1,0:T(8,128)(2,1)}, bf16[96,6144]{1,0:T(8,128)(2,1)}, u32[]{:S(2)}, u32[]{:S(2)}) collective-permute-start(bf16[96,6144]{1,0:T(8,128)(2,1)} %collective-permute-done.30.rest_1_), channel_id=1, source_target_pairs={{0,8},{2,10},{8,16},{10,18},{16,24},{18,26},{24,28},{26,30},{28,20... | collective-permute-start | bytes 3538952 | tf_op jit(solution)/shard_map/ppermute | solution.py:131
  102.5 27.0 %collective-permute-start.33 = (bf16[96,6144]{1,0:T(8,128)(2,1)}, bf16[96,6144]{1,0:T(8,128)(2,1)}, u32[]{:S(2)}, u32[]{:S(2)}) collective-permute-start(bf16[96,6144]{1,0:T(8,128)(2,1)} %collective-permute-done.31.rest_4_), channel_id=1, source_target_pairs={{8,0},{10,2},{16,8},{18,10},{24,16},{26,18},{28,24},{30,26},{20,28... | collective-permute-start | bytes 3538952 | tf_op jit(solution)/shard_map/ppermute | solution.py:132
  129.5 26.0 %collective-permute-start.35 = (bf16[96,6144]{1,0:T(8,128)(2,1)}, bf16[96,6144]{1,0:T(8,128)(2,1)}, u32[]{:S(2)}, u32[]{:S(2)}) collective-permute-start(bf16[96,6144]{1,0:T(8,128)(2,1)} %collective-permute-done.32.rest_2_), channel_id=1, source_target_pairs={{0,8},{2,10},{8,16},{10,18},{16,24},{18,26},{24,28},{26,30},{28,20... | collective-permute-start | bytes 3538952 | tf_op jit(solution)/shard_map/ppermute | solution.py:131
  130.2 25.7 %collective-permute-start.36 = (bf16[96,6144]{1,0:T(8,128)(2,1)}, bf16[96,6144]{1,0:T(8,128)(2,1)}, u32[]{:S(2)}, u32[]{:S(2)}) collective-permute-start(bf16[96,6144]{1,0:T(8,128)(2,1)} %collective-permute-done.33.rest_5_), channel_id=1, source_target_pairs={{8,0},{10,2},{16,8},{18,10},{24,16},{26,18},{28,24},{30,26},{20,28... | collective-permute-start | bytes 3538952 | tf_op jit(solution)/shard_map/ppermute | solution.py:132
  142.0 36.7 %collective-permute-start.39 = (bf16[512,1536]{1,0:T(8,128)(2,1)}, bf16[512,1536]{1,0:T(8,128)(2,1)}, u32[]{:S(2)}, u32[]{:S(2)}) collective-permute-start(bf16[512,1536]{1,0:T(8,128)(2,1)} %get-tuple-element.563.b_own.own_ref), channel_id=1, source_target_pairs={{0,1},{1,0},{2,3},{3,2},{4,5},{5,4},{6,7},{7,6},{8,9},{9,8},{10,11... | collective-permute-start | bytes 4718600 | tf_op jit(solution)/shard_map/ppermute | solution.py:35
  158.7 12.1 %collective-permute-start.37 = (bf16[96,3072]{1,0:T(8,128)(2,1)}, bf16[96,3072]{1,0:T(8,128)(2,1)S(1)}, u32[]{:S(2)}, u32[]{:S(2)}) collective-permute-start(bf16[96,3072]{1,0:T(8,128)(2,1)} %get-tuple-element.540), channel_id=1, source_target_pairs={{0,8},{2,10},{8,16},{10,18},{16,24},{18,26},{24,28},{26,30},{28,20... | collective-permute-start | bytes 1769480 | tf_op jit(solution)/shard_map/ppermute | solution.py:131
  159.2 11.9 %collective-permute-start.38 = (bf16[96,3072]{1,0:T(8,128)(2,1)}, bf16[96,3072]{1,0:T(8,128)(2,1)}, u32[]{:S(2)}, u32[]{:S(2)}) collective-permute-start(bf16[96,3072]{1,0:T(8,128)(2,1)} %get-tuple-element.541), channel_id=1, source_target_pairs={{8,0},{10,2},{16,8},{18,10},{24,16},{26,18},{28,24},{30,26},{20,28... | collective-permute-start | bytes 1769480 | tf_op jit(solution)/shard_map/ppermute | solution.py:132
  224.6 41.5 %collective-permute-start.40 = (bf16[512,1536]{1,0:T(8,128)(2,1)}, bf16[512,1536]{1,0:T(8,128)(2,1)}, u32[]{:S(2)}, u32[]{:S(2)}) collective-permute-start(bf16[512,1536]{1,0:T(8,128)(2,1)} %get-tuple-element.575), channel_id=1, source_target_pairs={{0,1},{1,0},{2,3},{3,2},{4,5},{5,4},{6,7},{7,6},{8,9},{9,8},{10,11... | collective-permute-start | bytes 4718600 | tf_op jit(solution)/shard_map/ppermute | solution.py:35
  249.4 16.7 %collective-permute-start.18 = (bf16[768,6144]{1,0:T(8,128)(2,1)}, bf16[768,6144]{1,0:T(8,128)(2,1)}, u32[]{:S(2)}, u32[]{:S(2)}) collective-permute-start(bf16[768,6144]{1,0:T(8,128)(2,1)} %products.4), channel_id=1, source_target_pairs={{0,2},{2,0},{4,6},{6,4},{8,10},{10,8},{12,14},{14,12},{16,18},{18,... | collective-permute-start | bytes 28311560 | tf_op jit(solution)/shard_map/cond/branch_1_fun/ppermute | solution.py:179
  273.0 37.1 %collective-permute-start.43 = (bf16[512,1536]{1,0:T(8,128)(2,1)}, bf16[512,1536]{1,0:T(8,128)(2,1)}, u32[]{:S(2)}, u32[]{:S(2)}) collective-permute-start(bf16[512,1536]{1,0:T(8,128)(2,1)} %get-tuple-element.603.left_ref.own_ref), channel_id=1, source_target_pairs={{0,1},{1,0},{2,3},{3,2},{4,5},{5,4},{6,7},{7,6},{8,9},{9,8},{10,11... | collective-permute-start | bytes 4718600 | tf_op jit(solution)/shard_map/ppermute | solution.py:35
  276.0 15.7 %collective-permute-start.41 = (bf16[96,3072]{1,0:T(8,128)(2,1)}, bf16[96,3072]{1,0:T(8,128)(2,1)S(1)}, u32[]{:S(2)}, u32[]{:S(2)}) collective-permute-start(bf16[96,3072]{1,0:T(8,128)(2,1)} %get-tuple-element.593), channel_id=1, source_target_pairs={{0,8},{2,10},{8,16},{10,18},{16,24},{18,26},{24,28},{26,30},{28,20... | collective-permute-start | bytes 1769480 | tf_op jit(solution)/shard_map/ppermute | solution.py:213
  276.7 15.5 %collective-permute-start.42 = (bf16[96,3072]{1,0:T(8,128)(2,1)}, bf16[96,3072]{1,0:T(8,128)(2,1)}, u32[]{:S(2)}, u32[]{:S(2)}) collective-permute-start(bf16[96,3072]{1,0:T(8,128)(2,1)} %get-tuple-element.594), channel_id=1, source_target_pairs={{8,0},{10,2},{16,8},{18,10},{24,16},{26,18},{28,24},{30,26},{20,28... | collective-permute-start | bytes 1769480 | tf_op jit(solution)/shard_map/ppermute | solution.py:214
  297.3 27.7 %collective-permute-start.44 = (bf16[96,6144]{1,0:T(8,128)(2,1)}, bf16[96,6144]{1,0:T(8,128)(2,1)}, u32[]{:S(2)}, u32[]{:S(2)}) collective-permute-start(bf16[96,6144]{1,0:T(8,128)(2,1)} %get-tuple-element.606), channel_id=1, source_target_pairs={{0,8},{2,10},{8,16},{10,18},{16,24},{18,26},{24,28},{26,30},{28,20... | collective-permute-start | bytes 3538952 | tf_op jit(solution)/shard_map/ppermute | solution.py:213
  298.0 27.4 %collective-permute-start.45 = (bf16[96,6144]{1,0:T(8,128)(2,1)}, bf16[96,6144]{1,0:T(8,128)(2,1)}, u32[]{:S(2)}, u32[]{:S(2)}) collective-permute-start(bf16[96,6144]{1,0:T(8,128)(2,1)} %get-tuple-element.607), channel_id=1, source_target_pairs={{8,0},{10,2},{16,8},{18,10},{24,16},{26,18},{28,24},{30,26},{20,28... | collective-permute-start | bytes 3538952 | tf_op jit(solution)/shard_map/ppermute | solution.py:214
  314.8 39.9 %collective-permute-start.46 = (bf16[512,1536]{1,0:T(8,128)(2,1)}, bf16[512,1536]{1,0:T(8,128)(2,1)}, u32[]{:S(2)}, u32[]{:S(2)}) collective-permute-start(bf16[512,1536]{1,0:T(8,128)(2,1)} %get-tuple-element.619), channel_id=1, source_target_pairs={{0,1},{1,0},{2,3},{3,2},{4,5},{5,4},{6,7},{7,6},{8,9},{9,8},{10,11... | collective-permute-start | bytes 4718600 | tf_op jit(solution)/shard_map/ppermute | solution.py:35
  330.5 33.5 %collective-permute-start.47 = (bf16[96,6144]{1,0:T(8,128)(2,1)}, bf16[96,6144]{1,0:T(8,128)(2,1)}, u32[]{:S(2)}, u32[]{:S(2)}) collective-permute-start(bf16[96,6144]{1,0:T(8,128)(2,1)} %get-tuple-element.626), channel_id=1, source_target_pairs={{0,8},{2,10},{8,16},{10,18},{16,24},{18,26},{24,28},{26,30},{28,20... | collective-permute-start | bytes 3538952 | tf_op jit(solution)/shard_map/ppermute | solution.py:213
  331.1 33.0 %collective-permute-start.48 = (bf16[96,6144]{1,0:T(8,128)(2,1)}, bf16[96,6144]{1,0:T(8,128)(2,1)}, u32[]{:S(2)}, u32[]{:S(2)}) collective-permute-start(bf16[96,6144]{1,0:T(8,128)(2,1)} %get-tuple-element.627), channel_id=1, source_target_pairs={{8,0},{10,2},{16,8},{18,10},{24,16},{26,18},{28,24},{30,26},{20,28... | collective-permute-start | bytes 3538952 | tf_op jit(solution)/shard_map/ppermute | solution.py:214
  369.1 32.8 %collective-permute-start.49 = (bf16[96,6144]{1,0:T(8,128)(2,1)}, bf16[96,6144]{1,0:T(8,128)(2,1)}, u32[]{:S(2)}, u32[]{:S(2)}) collective-permute-start(bf16[96,6144]{1,0:T(8,128)(2,1)} %get-tuple-element.650), channel_id=1, source_target_pairs={{0,8},{2,10},{8,16},{10,18},{16,24},{18,26},{24,28},{26,30},{28,20... | collective-permute-start | bytes 3538952 | tf_op jit(solution)/shard_map/ppermute | solution.py:213
  369.7 32.3 %collective-permute-start.50 = (bf16[96,6144]{1,0:T(8,128)(2,1)}, bf16[96,6144]{1,0:T(8,128)(2,1)}, u32[]{:S(2)}, u32[]{:S(2)}) collective-permute-start(bf16[96,6144]{1,0:T(8,128)(2,1)} %get-tuple-element.651), channel_id=1, source_target_pairs={{8,0},{10,2},{16,8},{18,10},{24,16},{26,18},{28,24},{30,26},{20,28... | collective-permute-start | bytes 3538952 | tf_op jit(solution)/shard_map/ppermute | solution.py:214
  374.9 38.2 %collective-permute-start.53 = (bf16[512,1536]{1,0:T(8,128)(2,1)}, bf16[512,1536]{1,0:T(8,128)(2,1)}, u32[]{:S(2)}, u32[]{:S(2)}) collective-permute-start(bf16[512,1536]{1,0:T(8,128)(2,1)} %get-tuple-element.702), channel_id=1, source_target_pairs={{0,1},{1,0},{2,3},{3,2},{4,5},{5,4},{6,7},{7,6},{8,9},{9,8},{10,11... | collective-permute-start | bytes 4718600 | tf_op jit(solution)/shard_map/ppermute | solution.py:35
  395.2 12.0 %collective-permute-start.51 = (bf16[96,1152]{1,0:T(8,128)(2,1)}, bf16[96,1152]{1,0:T(8,128)(2,1)S(1)}, u32[]{:S(2)}, u32[]{:S(2)}) collective-permute-start(bf16[96,1152]{1,0:T(8,128)(2,1)} %get-tuple-element.658), channel_id=1, source_target_pairs={{0,8},{2,10},{8,16},{10,18},{16,24},{18,26},{24,28},{26,30},{28,20... | collective-permute-start | bytes 663560 | tf_op jit(solution)/shard_map/ppermute | solution.py:213
  395.7 11.4 %collective-permute-start.52 = (bf16[96,1152]{1,0:T(8,128)(2,1)}, bf16[96,1152]{1,0:T(8,128)(2,1)S(1)}, u32[]{:S(2)}, u32[]{:S(2)}) collective-permute-start(bf16[96,1152]{1,0:T(8,128)(2,1)} %get-tuple-element.659), channel_id=1, source_target_pairs={{8,0},{10,2},{16,8},{18,10},{24,16},{26,18},{28,24},{30,26},{20,28... | collective-permute-start | bytes 663560 | tf_op jit(solution)/shard_map/ppermute | solution.py:214
  411.1 12.2 %collective-permute-start.54 = (bf16[96,2304]{1,0:T(8,128)(2,1)}, bf16[96,2304]{1,0:T(8,128)(2,1)S(1)}, u32[]{:S(2)}, u32[]{:S(2)}) collective-permute-start(bf16[96,2304]{1,0:T(8,128)(2,1)} %get-tuple-element.666), channel_id=1, source_target_pairs={{0,8},{2,10},{8,16},{10,18},{16,24},{18,26},{24,28},{26,30},{28,20... | collective-permute-start | bytes 1327112 | tf_op jit(solution)/shard_map/ppermute | solution.py:213
  411.6 11.9 %collective-permute-start.55 = (bf16[96,2304]{1,0:T(8,128)(2,1)}, bf16[96,2304]{1,0:T(8,128)(2,1)S(1)}, u32[]{:S(2)}, u32[]{:S(2)}) collective-permute-start(bf16[96,2304]{1,0:T(8,128)(2,1)} %get-tuple-element.667), channel_id=1, source_target_pairs={{8,0},{10,2},{16,8},{18,10},{24,16},{26,18},{28,24},{30,26},{20,28... | collective-permute-start | bytes 1327112 | tf_op jit(solution)/shard_map/ppermute | solution.py:214
  (44 other events, 259.4 us)
where the time goes:
time: 473 us; the launch traced here: 463 us
  Pallas kernels  261 us (55%)
  waiting for transfers between devices  119 us (25%)
  starting transfers between devices  48.2 us (10%)
  local copies, waits for them, and re-layouts  12.3 us (3%)
  other arithmetic  10.6 us (2%)
  matrix products  9.47 us (2%)
    pallas_call x4, Pallas kernels, products(): pl.pallas_call(functools.partial(products_kernel, starts, dims), grid=(st...  50.1 us
    pallas_call x1, Pallas kernels, ffn(): pl.pallas_call(functools.partial(ffn_kernel, columns, rows, ff), grid_spe...  45.9 us
    ppermute x8, waiting for transfers between devices, round(): self.behind.append(lax.ppermute(left, 'dp', forth))  40.5 us
    ppermute x18, waiting for transfers between devices, both(): return tuple((lax.ppermute(piece, 'dp', swap) for piece in pieces))  29.4 us
    pallas_call x8, Pallas kernels, combine(): pl.pallas_call(functools.partial(combine_kernel, edges), grid=(tiles,), i...  27.5 us
    ppermute x8, waiting for transfers between devices, round(): self.ahead = lax.ppermute(right, 'dp', forth)  27.2 us
    pallas_call x1, Pallas kernels, attend_back(): pl.pallas_call(backward_kernel, grid_spec=pltpu.PrefetchScalarGridSpec(nu...  21.9 us
    pallas_call x3, Pallas kernels, turned_product(): pl.pallas_call(turned_kernel, grid=(count,), in_specs=[spec((rows, depth)...  18.7 us
  transfers between devices with their start and end apart: 61, of which 43 were waited for; matrix products, arithmetic and copies ran while one was open for 5% of the time, Pallas kernels for 42%

commit v1 on v0

--- a/solution.py
+++ b/solution.py
@@ -17,7 +17,7 @@
 FAR = float(2**30)
 RING_LIMIT = 16
 TILE = 512
-VMEM = 66_000_000
+MIB = 2**20
 SCALE = 1.0 / math.sqrt(HEAD_DIM)
 LOG2E = math.log2(math.e)
 
@@ -339,7 +339,7 @@
         in_specs=[spec((rows, depth), lambda j: (0, 0)), spec((tile, depth), lambda j: (j, 0))],
         out_specs=[spec((rows // 2, tile), lambda j: (0, j))] * 2,
         out_shape=[jax.ShapeDtypeStruct((rows // 2, width), BF16)] * 2,
-        compiler_params=pltpu.CompilerParams(vmem_limit_bytes=VMEM),
+        compiler_params=pltpu.CompilerParams(vmem_limit_bytes=28 * MIB),
         cost_estimate=FREE,
         name="product",
     )(left, right)
@@ -388,7 +388,7 @@
         in_specs=in_specs,
         out_specs=spec((rows, tile), lambda j: (0, j)),
         out_shape=jax.ShapeDtypeStruct((rows, sum(widths)), BF16),
-        compiler_params=pltpu.CompilerParams(vmem_limit_bytes=VMEM),
+        compiler_params=pltpu.CompilerParams(vmem_limit_bytes=32 * MIB),
         cost_estimate=FREE,
         name="products",
     )(*lefts, *rights)
@@ -411,7 +411,7 @@
         ],
         out_specs=spec((tile, rows), lambda j: (j, 0)),
         out_shape=jax.ShapeDtypeStruct((count * tile, rows), BF16),
-        compiler_params=pltpu.CompilerParams(vmem_limit_bytes=VMEM),
+        compiler_params=pltpu.CompilerParams(vmem_limit_bytes=28 * MIB),
         cost_estimate=FREE,
         name="turned_product",
     )(left, right)
@@ -429,7 +429,7 @@
     return pl.pallas_call(
         join_kernel,
         out_shape=jax.ShapeDtypeStruct((rows, sum(part.shape[1] for part in parts)), BF16),
-        compiler_params=pltpu.CompilerParams(vmem_limit_bytes=VMEM),
+        compiler_params=pltpu.CompilerParams(vmem_limit_bytes=63 * MIB),
         cost_estimate=FREE,
         name="join",
     )(*parts)
@@ -448,7 +448,7 @@
             jax.ShapeDtypeStruct((rows, cut), left.dtype),
             jax.ShapeDtypeStruct((rows, width - cut), left.dtype),
         ],
-        compiler_params=pltpu.CompilerParams(vmem_limit_bytes=VMEM),
+        compiler_params=pltpu.CompilerParams(vmem_limit_bytes=63 * MIB),
         cost_estimate=FREE,
         name="halves",
     )(left, right)
@@ -483,7 +483,7 @@
         in_specs=[block] * len(arrays) + [pl.BlockSpec(gain.shape, lambda i: (0, 0))],
         out_specs=[block] * len(dtypes),
         out_shape=[jax.ShapeDtypeStruct((rows, width), dtype) for dtype in dtypes],
-        compiler_params=pltpu.CompilerParams(vmem_limit_bytes=VMEM),
+        compiler_params=pltpu.CompilerParams(vmem_limit_bytes=63 * MIB),
         cost_estimate=FREE,
         name=name,
     )(*arrays, gain)
@@ -526,7 +526,7 @@
         out_shape=[jax.ShapeDtypeStruct((rows, size), F32) for size in widths]
         + [jax.ShapeDtypeStruct((8, rows), F32)],
         scratch_shapes=[pltpu.VMEM((rows, 128), F32)],
-        compiler_params=pltpu.CompilerParams(vmem_limit_bytes=VMEM),
+        compiler_params=pltpu.CompilerParams(vmem_limit_bytes=28 * MIB),
         cost_estimate=FREE,
         name="finish",
     )(*parts, *weights)
@@ -563,7 +563,7 @@
         in_specs=in_specs,
         out_specs=[pl.BlockSpec((rows, tile), lambda j: (0, j)) for _ in outs],
         out_shape=[jax.ShapeDtypeStruct((rows, tiles * tile), dtype) for _ in outs],
-        compiler_params=pltpu.CompilerParams(vmem_limit_bytes=VMEM),
+        compiler_params=pltpu.CompilerParams(vmem_limit_bytes=16 * MIB),
         cost_estimate=FREE,
         name="combine",
     )(*arrays)
@@ -605,7 +605,7 @@
             scratch_shapes=[pltpu.VMEM((model, length), BF16)],
         ),
         out_shape=jax.ShapeDtypeStruct((model, length), BF16),
-        compiler_params=pltpu.CompilerParams(vmem_limit_bytes=VMEM),
+        compiler_params=pltpu.CompilerParams(vmem_limit_bytes=24 * MIB),
         cost_estimate=LONG,
         name="turn",
     )(turned, own, par)
@@ -658,7 +658,7 @@
             jax.ShapeDtypeStruct((model, qkv_width), BF16),
             jax.ShapeDtypeStruct((model, heads), BF16),
         ],
-        compiler_params=pltpu.CompilerParams(vmem_limit_bytes=VMEM),
+        compiler_params=pltpu.CompilerParams(vmem_limit_bytes=40 * MIB),
         cost_estimate=FREE,
         name="project",
     )(blocks, turned, x_own, x_par, cos, sin, *pieces)
@@ -784,7 +784,7 @@
             jax.ShapeDtypeStruct((half, model), BF16),
             jax.ShapeDtypeStruct((model, ff), BF16),
         ],
-        compiler_params=pltpu.CompilerParams(vmem_limit_bytes=VMEM),
+        compiler_params=pltpu.CompilerParams(vmem_limit_bytes=60 * MIB),
         cost_estimate=FREE,
         name="ffn",
     )(blocks, b_own, b_par, e_own, e_par, *pieces)
@@ -884,7 +884,7 @@
             jax.ShapeDtypeStruct((2 * groups * HEAD_DIM, length), BF16),
             jax.ShapeDtypeStruct((groups, 2, length), F32),
         ],
-        compiler_params=pltpu.CompilerParams(vmem_limit_bytes=VMEM),
+        compiler_params=pltpu.CompilerParams(vmem_limit_bytes=24 * MIB),
         cost_estimate=FREE,
         name="attend",
     )(side, qkv, qkv, qkv, doc_q, doc_k)
@@ -1015,7 +1015,7 @@
             ],
         ),
         out_shape=jax.ShapeDtypeStruct((hidden, length), BF16),
-        compiler_params=pltpu.CompilerParams(vmem_limit_bytes=VMEM),
+        compiler_params=pltpu.CompilerParams(vmem_limit_bytes=32 * MIB),
         cost_estimate=FREE,
         name="attend_back",
     )(side, qkv, qkv, qkv, att, *datt, lse, cos, sin, doc_q, doc_k)

time: 473 us -> 437 us (0.924)
  Pallas kernels: 261 us -> 222 us
  waiting for transfers between devices: 119 us -> 139 us
  other arithmetic: 10.6 us -> 3.46 us
  local copies, waits for them, and re-layouts: 12.3 us -> 6.78 us
    pallas_call x4, Pallas kernels: 50.1 us -> 38.9 us  [products(): pl.pallas_call(functools.partial(products_kernel, starts, dims), grid=(st...]
    pallas_call x3, Pallas kernels: 18.7 us -> 10.5 us  [turned_product(): pl.pallas_call(turned_kernel, grid=(count,), in_specs=[spec((rows, depth)...]
    ppermute x8, waiting for transfers between devices: 27.2 us -> 33.9 us  [round(): self.ahead = lax.ppermute(right, 'dp', forth)]
    pallas_call x3, Pallas kernels: 18.1 us -> 12.1 us  [turn(): pl.pallas_call(turn_kernel, grid_spec=pltpu.PrefetchScalarGridSpec(num_sc...]
    pallas_call x8, Pallas kernels: 27.5 us -> 21.8 us  [combine(): pl.pallas_call(functools.partial(combine_kernel, edges), grid=(tiles,), i...]
  transfers between devices with their start and end apart: 61 -> 61, of which waited for: 43 -> 46; matrix products, arithmetic and copies ran while one was open for 5% -> 3% of each run, Pallas kernels for 42% -> 36%
where the time goes in v1:
time: 437 us; the launch traced here: 429 us
  Pallas kernels  222 us (51%)
  waiting for transfers between devices  139 us (32%)
  starting transfers between devices  49 us (11%)
  local copies, waits for them, and re-layouts  6.78 us (2%)
  matrix products  5.7 us (1%)
    pallas_call x1, Pallas kernels, ffn(): pl.pallas_call(functools.partial(ffn_kernel, columns, rows, ff), grid_spe...  46 us
    ppermute x8, waiting for transfers between devices, round(): self.behind.append(lax.ppermute(left, 'dp', forth))  45 us
    pallas_call x4, Pallas kernels, products(): pl.pallas_call(functools.partial(products_kernel, starts, dims), grid=(st...  38.9 us
    ppermute x8, waiting for transfers between devices, round(): self.ahead = lax.ppermute(right, 'dp', forth)  33.9 us
    ppermute x18, waiting for transfers between devices, both(): return tuple((lax.ppermute(piece, 'dp', swap) for piece in pieces))  29.6 us
    pallas_call x1, Pallas kernels, attend_back(): pl.pallas_call(backward_kernel, grid_spec=pltpu.PrefetchScalarGridSpec(nu...  22 us
    pallas_call x8, Pallas kernels, combine(): pl.pallas_call(functools.partial(combine_kernel, edges), grid=(tiles,), i...  21.8 us
    ppermute x9, waiting for transfers between devices, swap_halves(): return lax.ppermute(value, 'tensor', [(0, 1), (1, 0)])  18.4 us
  transfers between devices with their start and end apart: 61, of which 46 were waited for; matrix products, arithmetic and copies ran while one was open for 3% of the time, Pallas kernels for 36%

profile of v1, /device:TPU:0, one launch (start us, length us, event | category | flops | bytes accessed | tf_op | source)
XLA Modules:
  0.0 428.9 jit_solution(15111742129798211172)
XLA Ops:
  24.4 6.7 %collective-permute-done.22.rest_2_ = bf16[96,2432]{1,0:T(8,128)(2,1)} collective-permute-done((bf16[96,2432]{1,0:T(8,128)(2,1)}, bf16[96,2432]{1,0:T(8,128)(2,1)}, u32[]{:S(2)}, u32[]{:S(2)}) %collective-permute-start.22) | collective-permute-done | bytes 466976 | tf_op jit(solution)/shard_map/ppermute | solution.py:131
  37.4 5.3 %collective-permute-done.24.left_ref.rest_3_ = bf16[96,2432]{1,0:T(8,128)(2,1)S(1)} collective-permute-done((bf16[96,2432]{1,0:T(8,128)(2,1)}, bf16[96,2432]{1,0:T(8,128)(2,1)S(1)}, u32[]{:S(2)}, u32[]{:S(2)}) %collective-permute-start.24) | collective-permute-done | bytes 466976 | tf_op jit(solution)/shard_map/ppermute | solution.py:131
  60.1 17.0 %project.1 = (bf16[1536,1024]{1,0:T(8,128)(2,1)S(1)}, f32[8,1536]{1,0:T(8,128)S(1)}, bf16[1536,1024]{1,0:T(8,128)(2,1)}, bf16[1536,1536]{1,0:T(8,128)(2,1)S(1)}, bf16[1536,768]{1,0:T(8,128)(2,1)S(1)}) custom-call(s32[18]{0:T(128)S(1)} %pad_add_fusion.block_ref, s32[16]{0:T(128)S(1)} %pad_add_fusion.1.turn_ref, bf16[512,1536]{1,0:T(8,128)(2,1)S(1)} %bitcast.37, ...), custom_call_target="tpu_custom_call" | custom-call | tf_op jit(solution)/shard_map/project/pallas_call | solution.py:626
  79.3 12.9 %attend.1 = (bf16[768,1024]{1,0:T(8,128)(2,1)S(1)}, f32[4,2,1024]{2,1,0:T(2,128)S(1)}) custom-call(s32[1]{0:T(128)} %bitcast.8.side_ref, bf16[1536,1024]{1,0:T(8,128)(2,1)S(1)} %get-tuple-element.611.q_in.k_in.v_in.q_ref.k_ref.v_ref, bf16[1536,1024]{1,0:T(8,128)(2,1)S(1)} %get-tuple-element.611.q_in.k_in.v_in.q_ref.k_ref.v_ref, ...), custom_call_target="tpu_custom_call" | custom-call | tf_op jit(solution)/shard_map/attend/pallas_call | solution.py:866
  98.2 5.1 %conditional.18 = (bf16[96,6144]{1,0:T(8,128)(2,1)}, bf16[96,6144]{1,0:T(8,128)(2,1)}) conditional(s32[]{:T(128)} %bitcast.3, () %tuple.245, (bf16[96,6144]{1,0:T(8,128)(2,1)}, bf16[96,6144]{1,0:T(8,128)(2,1)}) %tuple.247), branch_computations={%region_12.13_spmd, %region_13.14_spmd} | conditional | bytes 9437280 | solution.py:118
  110.4 13.0 %collective-permute-done.32.rest_2_ = bf16[96,6144]{1,0:T(8,128)(2,1)} collective-permute-done((bf16[96,6144]{1,0:T(8,128)(2,1)}, bf16[96,6144]{1,0:T(8,128)(2,1)}, u32[]{:S(2)}, u32[]{:S(2)}) %collective-permute-start.32) | collective-permute-done | bytes 1179680 | tf_op jit(solution)/shard_map/ppermute | solution.py:131
  126.6 4.9 %conditional.19 = (bf16[96,6144]{1,0:T(8,128)(2,1)}, bf16[96,6144]{1,0:T(8,128)(2,1)}) conditional(s32[]{:T(128)} %bitcast.3, () %tuple.255, (bf16[96,6144]{1,0:T(8,128)(2,1)}, bf16[96,6144]{1,0:T(8,128)(2,1)}) %tuple.257), branch_computations={%region_14.15_spmd, %region_15.16_spmd} | conditional | bytes 9437280 | solution.py:118
  131.5 5.6 %residual.1 = (f32[512,1536]{1,0:T(8,128)}, bf16[512,1536]{1,0:T(8,128)(2,1)}) custom-call(f32[512,1536]{1,0:T(8,128)} %fusion.part_ref, bf16[512,1536]{1,0:T(8,128)(2,1)} %collective-permute-done.34.sent_ref, bf16[512,1536]{1,0:T(8,128)(2,1)} %bitcast.35, f32[8,1536]{1,0:T(8,128)} %copy-done.17), custom_call_target="tpu_custom_call" | custom-call | tf_op jit(solution)/shard_map/residual/pallas_call | solution.py:480
  137.9 12.7 %collective-permute-done.35.left_ref.rest_3_ = bf16[96,6144]{1,0:T(8,128)(2,1)} collective-permute-done((bf16[96,6144]{1,0:T(8,128)(2,1)}, bf16[96,6144]{1,0:T(8,128)(2,1)}, u32[]{:S(2)}, u32[]{:S(2)}) %collective-permute-start.35) | collective-permute-done | bytes 1179680 | tf_op jit(solution)/shard_map/ppermute | solution.py:131
  155.8 4.9 %conditional.20 = (bf16[96,6144]{1,0:T(8,128)(2,1)}, bf16[96,6144]{1,0:T(8,128)(2,1)}) conditional(s32[]{:T(128)} %bitcast.3, () %tuple.263, (bf16[96,6144]{1,0:T(8,128)(2,1)}, bf16[96,6144]{1,0:T(8,128)(2,1)}) %tuple.265), branch_computations={%region_16.17_spmd, %region_17.18_spmd} | conditional | bytes 9437280 | solution.py:118
  160.7 5.2 %collective-permute-done.37.rest_7_ = bf16[96,3072]{1,0:T(8,128)(2,1)S(1)} collective-permute-done((bf16[96,3072]{1,0:T(8,128)(2,1)}, bf16[96,3072]{1,0:T(8,128)(2,1)S(1)}, u32[]{:S(2)}, u32[]{:S(2)}) %collective-permute-start.37) | collective-permute-done | bytes 589856 | tf_op jit(solution)/shard_map/ppermute | solution.py:131
  169.5 4.4 %collective-permute-done.39.b_par.par_ref = bf16[512,1536]{1,0:T(8,128)(2,1)} collective-permute-done((bf16[512,1536]{1,0:T(8,128)(2,1)}, bf16[512,1536]{1,0:T(8,128)(2,1)}, u32[]{:S(2)}, u32[]{:S(2)}) %collective-permute-start.39) | collective-permute-done | bytes 1572896 | tf_op jit(solution)/shard_map/ppermute | solution.py:35
  173.8 46.0 %ffn.1 = (bf16[1024,2048]{1,0:T(8,128)(2,1)}, bf16[1024,4096]{1,0:T(8,128)(2,1)}, f32[512,1536]{1,0:T(8,128)}, bf16[512,1536]{1,0:T(8,128)(2,1)}, bf16[1536,2048]{1,0:T(8,128)(2,1)}) custom-call(s32[18]{0:T(128)} %copy-done.24, bf16[512,1536]{1,0:T(8,128)(2,1)} %get-tuple-element.563.b_own.own_ref, bf16[512,1536]{1,0:T(8,128)(2,1)} %collective-permute-done.39.b_par.par_ref, ...), custom_call_target="tpu_custom_call" | custom-call | tf_op jit(solution)/shard_map/ffn/pallas_call | solution.py:758
  220.7 5.7 %turn.4 = bf16[1536,1024]{1,0:T(8,128)(2,1)} custom-call(s32[16]{0:T(128)S(1)} %pad_add_fusion.1.turn_ref, bf16[512,1536]{1,0:T(8,128)(2,1)S(1)} %copy-done.10, bf16[512,1536]{1,0:T(8,128)(2,1)} %collective-permute-done.39.b_par.par_ref), custom_call_target="tpu_custom_call" | custom-call | bytes 41943040 | tf_op jit(solution)/shard_map/turn/pallas_call | solution.py:598
  226.5 30.9 %conditional.22 = (bf16[768,6144]{1,0:T(8,128)(2,1)}, bf16[768,6144]{1,0:T(8,128)(2,1)}) conditional(s32[]{:T(128)} %bitcast.3, () %tuple.275, (bf16[1536,1024]{1,0:T(8,128)(2,1)}, bf16[1536,1024]{1,0:T(8,128)(2,1)}, bf16[1024,2048]{1,0:T(8,128)(2,1)S(1)}, bf16[1024,4096]{1,0:T(8,128)(2,1)}) %tuple.356), branch_computations={%region_20.21_spmd, %region_21.22_spmd} | conditional | bytes 96469128 | solution.py:187
  227.0 15.6 %products.4 = bf16[768,6144]{1,0:T(8,128)(2,1)S(1)} custom-call(bf16[1536,1024]{1,0:T(8,128)(2,1)} %get-tuple-element.72.refs_0_, bf16[1536,1024]{1,0:T(8,128)(2,1)} %get-tuple-element.73.refs_1_, bf16[1024,2048]{1,0:T(8,128)(2,1)S(1)} %get-tuple-element.78.refs_2_, bf16[1024,4096]{1,0:T(8,128)(2,1)} %get-tuple-element.79.refs_3_), custom_call_target="tpu_custom_call" | custom-call | tf_op jit(solution)/shard_map/cond/branch_1_fun/products/pallas_call | solution.py:385
  242.6 14.2 %products.5 = bf16[768,6144]{1,0:T(8,128)(2,1)} custom-call(bf16[1536,1024]{1,0:T(8,128)(2,1)S(1)} %copy-done.30, bf16[1536,1024]{1,0:T(8,128)(2,1)S(1)} %copy-done.31, bf16[1024,2048]{1,0:T(8,128)(2,1)S(1)} %get-tuple-element.78.refs_2_, bf16[1024,4096]{1,0:T(8,128)(2,1)S(1)} %copy-done.29), custom_call_target="tpu_custom_call" | custom-call | tf_op jit(solution)/shard_map/cond/branch_1_fun/products/pallas_call | solution.py:385
  257.4 6.8 %norm_back.2 = (f32[512,1536]{1,0:T(8,128)}, bf16[512,1536]{1,0:T(8,128)(2,1)}) custom-call(f32[512,1536]{1,0:T(8,128)} %get-tuple-element.574.own_ref, bf16[512,1536]{1,0:T(8,128)(2,1)} %collective-permute-done.40.sent_ref, f32[512,1536]{1,0:T(8,128)} %get-tuple-element.577.value_ref, bf16[512,1536]{1,0:T(8,128)(2,1)} %bitcast.39, f32[8,1536]{1,0:T(8,128)} %copy-done.17), custom_call_target="tpu_custom_call" | custom-call | tf_op jit(solution)/shard_map/norm_back/pallas_call | solution.py:480
  269.9 8.3 %product.1 = (bf16[512,1536]{1,0:T(8,128)(2,1)S(1)}, bf16[512,1536]{1,0:T(8,128)(2,1)S(1)}) custom-call(bf16[1024,2048]{1,0:T(8,128)(2,1)S(1)} %copy-done.28, bf16[1536,2048]{1,0:T(8,128)(2,1)S(1)} %bitcast.43), custom_call_target="tpu_custom_call" | custom-call | tf_op jit(solution)/shard_map/product/pallas_call | solution.py:336
  278.2 4.7 %collective-permute-done.41.refs_2_ = bf16[96,3072]{1,0:T(8,128)(2,1)S(1)} collective-permute-done((bf16[96,3072]{1,0:T(8,128)(2,1)S(1)}, bf16[96,3072]{1,0:T(8,128)(2,1)S(1)}, u32[]{:S(2)}, u32[]{:S(2)}) %collective-permute-start.41) | collective-permute-done | bytes 589856 | tf_op jit(solution)/shard_map/ppermute | solution.py:213
  291.5 9.4 %collective-permute-done.43.left_ref.par_ref = bf16[512,1536]{1,0:T(8,128)(2,1)S(1)} collective-permute-done((bf16[512,1536]{1,0:T(8,128)(2,1)}, bf16[512,1536]{1,0:T(8,128)(2,1)S(1)}, u32[]{:S(2)}, u32[]{:S(2)}) %collective-permute-start.43) | collective-permute-done | bytes 1572896 | tf_op jit(solution)/shard_map/ppermute | solution.py:35
  306.9 6.6 %collective-permute-done.44.refs_2_ = bf16[96,6144]{1,0:T(8,128)(2,1)S(1)} collective-permute-done((bf16[96,6144]{1,0:T(8,128)(2,1)S(1)}, bf16[96,6144]{1,0:T(8,128)(2,1)S(1)}, u32[]{:S(2)}, u32[]{:S(2)}) %collective-permute-start.44) | collective-permute-done | bytes 1179680 | tf_op jit(solution)/shard_map/ppermute | solution.py:213
  319.7 22.0 %attend_back.1.right_ref = bf16[1536,1024]{1,0:T(8,128)(2,1)S(1)} custom-call(s32[1]{0:T(128)} %bitcast.8.side_ref, bf16[1536,1024]{1,0:T(8,128)(2,1)S(1)} %copy-done.1, bf16[1536,1024]{1,0:T(8,128)(2,1)S(1)} %copy-done.1, bf16[1536,1024]{1,0:T(8,128)(2,1)S(1)} %copy-done.1, bf16[768,1024]{1,0:T(8,128)(2,1)S(1)} %copy-done.34, ...), custom_call_target="tpu_custom_call" | custom-call | tf_op jit(solution)/shard_map/attend_back/pallas_call | solution.py:1001
  341.7 5.8 %turned_product.5 = bf16[1024,1536]{1,0:T(8,128)(2,1)S(1)} custom-call(bf16[1536,1536]{1,0:T(8,128)(2,1)S(1)} %bitcast.45, bf16[1536,1024]{1,0:T(8,128)(2,1)S(1)} %attend_back.1.right_ref), custom_call_target="tpu_custom_call" | custom-call | tf_op jit(solution)/shard_map/turned_product/pallas_call | solution.py:405
  347.5 4.6 %combine.11 = (bf16[96,6144]{1,0:T(8,128)(2,1)}, bf16[96,6144]{1,0:T(8,128)(2,1)}) custom-call(bf16[768,6144]{1,0:T(8,128)(2,1)} %get-tuple-element.649.refs_0_.refs_2_.refs_3_, bf16[768,6144]{1,0:T(8,128)(2,1)} %get-tuple-element.583.refs_1_.refs_3_.refs_4_, bf16[96,6144]{1,0:T(8,128)(2,1)S(1)} %collective-permute-done.47.refs_2_, ...), custom_call_target="tpu_custom_call" | custom-call | tf_op jit(solution)/shard_map/combine/pallas_call | solution.py:560
  356.8 11.0 %conditional.23 = (bf16[768,2304]{1,0:T(8,128)(2,1)}, bf16[768,2304]{1,0:T(8,128)(2,1)S(1)}) conditional(s32[]{:T(128)} %bitcast.3, () %tuple.303, (bf16[1536,1024]{1,0:T(8,128)(2,1)S(1)}, bf16[1536,1024]{1,0:T(8,128)(2,1)S(1)}, bf16[1536,1024]{1,0:T(8,128)(2,1)S(1)}, bf16[768,1024]{1,0:T(8,128)(2,1)S(1)}) %tuple.358), branch_computations={%region_22.23_spmd, %region_23.24_spmd} | conditional | bytes 14155832 | solution.py:187
  356.8 4.6 %products.6 = bf16[768,2304]{1,0:T(8,128)(2,1)S(1)} custom-call(bf16[1536,1024]{1,0:T(8,128)(2,1)S(1)} %get-tuple-element.80.refs_0_, bf16[1536,1024]{1,0:T(8,128)(2,1)S(1)} %get-tuple-element.81.refs_1_, bf16[1536,1024]{1,0:T(8,128)(2,1)S(1)} %get-tuple-element.86.refs_2_, bf16[768,1024]{1,0:T(8,128)(2,1)S(1)} %get-tuple-element.87.refs_3_), custom_call_target="tpu_custom_call" | custom-call | tf_op jit(solution)/shard_map/cond/branch_1_fun/products/pallas_call | solution.py:385
  361.4 4.6 %products.7 = bf16[768,2304]{1,0:T(8,128)(2,1)S(1)} custom-call(bf16[1536,1024]{1,0:T(8,128)(2,1)S(1)} %get-tuple-element.80.refs_0_, bf16[1536,1024]{1,0:T(8,128)(2,1)S(1)} %get-tuple-element.81.refs_1_, bf16[1536,1024]{1,0:T(8,128)(2,1)S(1)} %get-tuple-element.86.refs_2_, bf16[768,1024]{1,0:T(8,128)(2,1)S(1)} %get-tuple-element.87.refs_3_), custom_call_target="tpu_custom_call" | custom-call | tf_op jit(solution)/shard_map/cond/branch_1_fun/products/pallas_call | solution.py:385
  373.7 5.7 %collective-permute-done.49.refs_2_ = bf16[96,6144]{1,0:T(8,128)(2,1)S(1)} collective-permute-done((bf16[96,6144]{1,0:T(8,128)(2,1)}, bf16[96,6144]{1,0:T(8,128)(2,1)S(1)}, u32[]{:S(2)}, u32[]{:S(2)}) %collective-permute-start.49) | collective-permute-done | bytes 1179680 | tf_op jit(solution)/shard_map/ppermute | solution.py:213
  389.0 6.7 %collective-permute-done.54.refs_2_ = bf16[96,2304]{1,0:T(8,128)(2,1)S(1)} collective-permute-done((bf16[96,2304]{1,0:T(8,128)(2,1)S(1)}, bf16[96,2304]{1,0:T(8,128)(2,1)S(1)}, u32[]{:S(2)}, u32[]{:S(2)}) %collective-permute-start.54) | collective-permute-done | bytes 442400 | tf_op jit(solution)/shard_map/ppermute | solution.py:213
  400.6 5.6 %norm_back.3 = bf16[512,1536]{1,0:T(8,128)(2,1)} custom-call(bf16[512,1536]{1,0:T(8,128)(2,1)} %get-tuple-element.671.own_ref, bf16[512,1536]{1,0:T(8,128)(2,1)} %collective-permute-done.53.sent_ref, bf16[512,1536]{1,0:T(8,128)(2,1)} %bitcast.36, f32[512,1536]{1,0:T(8,128)} %get-tuple-element.673.base_ref, f32[8,1536]{1,0:T(8,128)} %copy-done.17), custom_call_target="tpu_custom_call" | custom-call | tf_op jit(solution)/shard_map/norm_back/pallas_call | solution.py:480
  414.6 6.2 %collective-permute-done.58.refs_2_ = bf16[96,2304]{1,0:T(8,128)(2,1)S(1)} collective-permute-done((bf16[96,2304]{1,0:T(8,128)(2,1)S(1)}, bf16[96,2304]{1,0:T(8,128)(2,1)S(1)}, u32[]{:S(2)}, u32[]{:S(2)}) %collective-permute-start.58) | collective-permute-done | bytes 442400 | tf_op jit(solution)/shard_map/ppermute | solution.py:213
  (264 shorter events, 180.0 us)
Async XLA Ops:
  4.1 13.9 %collective-permute-start.20 = (bf16[96,2432]{1,0:T(8,128)(2,1)}, bf16[96,2432]{1,0:T(8,128)(2,1)}, u32[]{:S(2)}, u32[]{:S(2)}) collective-permute-start(bf16[96,2432]{1,0:T(8,128)(2,1)} %join.2.rest_0_), channel_id=1, source_target_pairs={{0,8},{2,10},{8,16},{10,18},{16,24},{18,26},{24,28},{26,30},{28,20... | collective-permute-start | bytes 1400840 | tf_op jit(solution)/shard_map/ppermute | solution.py:131
  7.1 12.5 %collective-permute-start.21 = (bf16[96,2432]{1,0:T(8,128)(2,1)}, bf16[96,2432]{1,0:T(8,128)(2,1)}, u32[]{:S(2)}, u32[]{:S(2)}) collective-permute-start(bf16[96,2432]{1,0:T(8,128)(2,1)} %join.2.rest_0_), channel_id=1, source_target_pairs={{8,0},{10,2},{16,8},{18,10},{24,16},{26,18},{28,24},{30,26},{20,28... | collective-permute-start | bytes 1400840 | tf_op jit(solution)/shard_map/ppermute | solution.py:132
  7.1 48.3 %collective-permute-start.28 = (bf16[512,1536]{1,0:T(8,128)(2,1)}, bf16[512,1536]{1,0:T(8,128)(2,1)}, u32[]{:S(2)}, u32[]{:S(2)}) collective-permute-start(bf16[512,1536]{1,0:T(8,128)(2,1)} %bitcast.34), channel_id=1, source_target_pairs={{0,1},{1,0},{2,3},{3,2},{4,5},{5,4},{6,7},{7,6},{8,9},{9,8},{10,11... | collective-permute-start | bytes 4718600 | tf_op jit(solution)/shard_map/ppermute | solution.py:35
  19.6 11.6 %collective-permute-start.22 = (bf16[96,2432]{1,0:T(8,128)(2,1)}, bf16[96,2432]{1,0:T(8,128)(2,1)}, u32[]{:S(2)}, u32[]{:S(2)}) collective-permute-start(bf16[96,2432]{1,0:T(8,128)(2,1)} %collective-permute-done.20.rest_1_), channel_id=1, source_target_pairs={{0,8},{2,10},{8,16},{10,18},{16,24},{18,26},{24,28},{26,30},{28,20... | collective-permute-start | bytes 1400840 | tf_op jit(solution)/shard_map/ppermute | solution.py:131
  55.4 36.9 %collective-permute-start.29 = (bf16[512,1536]{1,0:T(8,128)(2,1)S(1)}, bf16[512,1536]{1,0:T(8,128)(2,1)S(1)}, u32[]{:S(2)}, u32[]{:S(2)}) collective-permute-start(bf16[512,1536]{1,0:T(8,128)(2,1)S(1)} %bitcast.40), channel_id=1, source_target_pairs={{0,1},{1,0},{2,3},{3,2},{4,5},{5,4},{6,7},{7,6},{8,9},{9,8},{10,11... | collective-permute-start | bytes 4718600 | tf_op jit(solution)/shard_map/ppermute | solution.py:35
  57.0 39.1 %collective-permute-start.30 = (bf16[96,6144]{1,0:T(8,128)(2,1)}, bf16[96,6144]{1,0:T(8,128)(2,1)}, u32[]{:S(2)}, u32[]{:S(2)}) collective-permute-start(bf16[96,6144]{1,0:T(8,128)(2,1)} %join.3.rest_0_), channel_id=1, source_target_pairs={{0,8},{2,10},{8,16},{10,18},{16,24},{18,26},{24,28},{26,30},{28,20... | collective-permute-start | bytes 3538952 | tf_op jit(solution)/shard_map/ppermute | solution.py:131
  58.6 37.5 %collective-permute-start.31 = (bf16[96,6144]{1,0:T(8,128)(2,1)}, bf16[96,6144]{1,0:T(8,128)(2,1)}, u32[]{:S(2)}, u32[]{:S(2)}) collective-permute-start(bf16[96,6144]{1,0:T(8,128)(2,1)} %join.3.rest_0_), channel_id=1, source_target_pairs={{8,0},{10,2},{16,8},{18,10},{24,16},{26,18},{28,24},{30,26},{20,28... | collective-permute-start | bytes 3538952 | tf_op jit(solution)/shard_map/ppermute | solution.py:132
  94.9 36.6 %collective-permute-start.34 = (bf16[512,1536]{1,0:T(8,128)(2,1)}, bf16[512,1536]{1,0:T(8,128)(2,1)}, u32[]{:S(2)}, u32[]{:S(2)}) collective-permute-start(bf16[512,1536]{1,0:T(8,128)(2,1)} %convolution_convert_fusion), channel_id=1, source_target_pairs={{0,1},{1,0},{2,3},{3,2},{4,5},{5,4},{6,7},{7,6},{8,9},{9,8},{10,11... | collective-permute-start | bytes 4718600 | tf_op jit(solution)/shard_map/ppermute | solution.py:35
  96.1 27.3 %collective-permute-start.32 = (bf16[96,6144]{1,0:T(8,128)(2,1)}, bf16[96,6144]{1,0:T(8,128)(2,1)}, u32[]{:S(2)}, u32[]{:S(2)}) collective-permute-start(bf16[96,6144]{1,0:T(8,128)(2,1)} %collective-permute-done.30.rest_1_), channel_id=1, source_target_pairs={{0,8},{2,10},{8,16},{10,18},{16,24},{18,26},{24,28},{26,30},{28,20... | collective-permute-start | bytes 3538952 | tf_op jit(solution)/shard_map/ppermute | solution.py:131
  97.6 27.0 %collective-permute-start.33 = (bf16[96,6144]{1,0:T(8,128)(2,1)}, bf16[96,6144]{1,0:T(8,128)(2,1)}, u32[]{:S(2)}, u32[]{:S(2)}) collective-permute-start(bf16[96,6144]{1,0:T(8,128)(2,1)} %collective-permute-done.31.rest_4_), channel_id=1, source_target_pairs={{8,0},{10,2},{16,8},{18,10},{24,16},{26,18},{28,24},{30,26},{20,28... | collective-permute-start | bytes 3538952 | tf_op jit(solution)/shard_map/ppermute | solution.py:132
  124.6 26.0 %collective-permute-start.35 = (bf16[96,6144]{1,0:T(8,128)(2,1)}, bf16[96,6144]{1,0:T(8,128)(2,1)}, u32[]{:S(2)}, u32[]{:S(2)}) collective-permute-start(bf16[96,6144]{1,0:T(8,128)(2,1)} %collective-permute-done.32.rest_2_), channel_id=1, source_target_pairs={{0,8},{2,10},{8,16},{10,18},{16,24},{18,26},{24,28},{26,30},{28,20... | collective-permute-start | bytes 3538952 | tf_op jit(solution)/shard_map/ppermute | solution.py:131
  125.4 25.8 %collective-permute-start.36 = (bf16[96,6144]{1,0:T(8,128)(2,1)}, bf16[96,6144]{1,0:T(8,128)(2,1)}, u32[]{:S(2)}, u32[]{:S(2)}) collective-permute-start(bf16[96,6144]{1,0:T(8,128)(2,1)} %collective-permute-done.33.rest_5_), channel_id=1, source_target_pairs={{8,0},{10,2},{16,8},{18,10},{24,16},{26,18},{28,24},{30,26},{20,28... | collective-permute-start | bytes 3538952 | tf_op jit(solution)/shard_map/ppermute | solution.py:132
  137.1 36.8 %collective-permute-start.39 = (bf16[512,1536]{1,0:T(8,128)(2,1)}, bf16[512,1536]{1,0:T(8,128)(2,1)}, u32[]{:S(2)}, u32[]{:S(2)}) collective-permute-start(bf16[512,1536]{1,0:T(8,128)(2,1)} %get-tuple-element.563.b_own.own_ref), channel_id=1, source_target_pairs={{0,1},{1,0},{2,3},{3,2},{4,5},{5,4},{6,7},{7,6},{8,9},{9,8},{10,11... | collective-permute-start | bytes 4718600 | tf_op jit(solution)/shard_map/ppermute | solution.py:35
  153.8 12.1 %collective-permute-start.37 = (bf16[96,3072]{1,0:T(8,128)(2,1)}, bf16[96,3072]{1,0:T(8,128)(2,1)S(1)}, u32[]{:S(2)}, u32[]{:S(2)}) collective-permute-start(bf16[96,3072]{1,0:T(8,128)(2,1)} %get-tuple-element.540), channel_id=1, source_target_pairs={{0,8},{2,10},{8,16},{10,18},{16,24},{18,26},{24,28},{26,30},{28,20... | collective-permute-start | bytes 1769480 | tf_op jit(solution)/shard_map/ppermute | solution.py:131
  154.4 11.9 %collective-permute-start.38 = (bf16[96,3072]{1,0:T(8,128)(2,1)}, bf16[96,3072]{1,0:T(8,128)(2,1)}, u32[]{:S(2)}, u32[]{:S(2)}) collective-permute-start(bf16[96,3072]{1,0:T(8,128)(2,1)} %get-tuple-element.541), channel_id=1, source_target_pairs={{8,0},{10,2},{16,8},{18,10},{24,16},{26,18},{28,24},{30,26},{20,28... | collective-permute-start | bytes 1769480 | tf_op jit(solution)/shard_map/ppermute | solution.py:132
  219.8 37.6 %collective-permute-start.40 = (bf16[512,1536]{1,0:T(8,128)(2,1)}, bf16[512,1536]{1,0:T(8,128)(2,1)}, u32[]{:S(2)}, u32[]{:S(2)}) collective-permute-start(bf16[512,1536]{1,0:T(8,128)(2,1)} %get-tuple-element.575), channel_id=1, source_target_pairs={{0,1},{1,0},{2,3},{3,2},{4,5},{5,4},{6,7},{7,6},{8,9},{9,8},{10,11... | collective-permute-start | bytes 4718600 | tf_op jit(solution)/shard_map/ppermute | solution.py:35
  242.5 14.9 %collective-permute-start.18 = (bf16[768,6144]{1,0:T(8,128)(2,1)S(1)}, bf16[768,6144]{1,0:T(8,128)(2,1)}, u32[]{:S(2)}, u32[]{:S(2)}) collective-permute-start(bf16[768,6144]{1,0:T(8,128)(2,1)S(1)} %products.4), channel_id=1, source_target_pairs={{0,2},{2,0},{4,6},{6,4},{8,10},{10,8},{12,14},{14,12},{16,18},{18,... | collective-permute-start | bytes 28311560 | tf_op jit(solution)/shard_map/cond/branch_1_fun/ppermute | solution.py:179
  264.2 36.7 %collective-permute-start.43 = (bf16[512,1536]{1,0:T(8,128)(2,1)}, bf16[512,1536]{1,0:T(8,128)(2,1)S(1)}, u32[]{:S(2)}, u32[]{:S(2)}) collective-permute-start(bf16[512,1536]{1,0:T(8,128)(2,1)} %get-tuple-element.603.left_ref.own_ref), channel_id=1, source_target_pairs={{0,1},{1,0},{2,3},{3,2},{4,5},{5,4},{6,7},{7,6},{8,9},{9,8},{10,11... | collective-permute-start | bytes 4718600 | tf_op jit(solution)/shard_map/ppermute | solution.py:35
  267.8 15.0 %collective-permute-start.41 = (bf16[96,3072]{1,0:T(8,128)(2,1)S(1)}, bf16[96,3072]{1,0:T(8,128)(2,1)S(1)}, u32[]{:S(2)}, u32[]{:S(2)}) collective-permute-start(bf16[96,3072]{1,0:T(8,128)(2,1)S(1)} %get-tuple-element.593), channel_id=1, source_target_pairs={{0,8},{2,10},{8,16},{10,18},{16,24},{18,26},{24,28},{26,30},{28,20... | collective-permute-start | bytes 1769480 | tf_op jit(solution)/shard_map/ppermute | solution.py:213
  268.6 14.7 %collective-permute-start.42 = (bf16[96,3072]{1,0:T(8,128)(2,1)S(1)}, bf16[96,3072]{1,0:T(8,128)(2,1)S(1)}, u32[]{:S(2)}, u32[]{:S(2)}) collective-permute-start(bf16[96,3072]{1,0:T(8,128)(2,1)S(1)} %get-tuple-element.594), channel_id=1, source_target_pairs={{8,0},{10,2},{16,8},{18,10},{24,16},{26,18},{28,24},{30,26},{20,28... | collective-permute-start | bytes 1769480 | tf_op jit(solution)/shard_map/ppermute | solution.py:214
  287.0 26.5 %collective-permute-start.44 = (bf16[96,6144]{1,0:T(8,128)(2,1)S(1)}, bf16[96,6144]{1,0:T(8,128)(2,1)S(1)}, u32[]{:S(2)}, u32[]{:S(2)}) collective-permute-start(bf16[96,6144]{1,0:T(8,128)(2,1)S(1)} %get-tuple-element.606), channel_id=1, source_target_pairs={{0,8},{2,10},{8,16},{10,18},{16,24},{18,26},{24,28},{26,30},{28,20... | collective-permute-start | bytes 3538952 | tf_op jit(solution)/shard_map/ppermute | solution.py:213
  287.6 26.2 %collective-permute-start.45 = (bf16[96,6144]{1,0:T(8,128)(2,1)S(1)}, bf16[96,6144]{1,0:T(8,128)(2,1)S(1)}, u32[]{:S(2)}, u32[]{:S(2)}) collective-permute-start(bf16[96,6144]{1,0:T(8,128)(2,1)S(1)} %get-tuple-element.607), channel_id=1, source_target_pairs={{8,0},{10,2},{16,8},{18,10},{24,16},{26,18},{28,24},{30,26},{20,28... | collective-permute-start | bytes 3538952 | tf_op jit(solution)/shard_map/ppermute | solution.py:214
  303.3 38.4 %collective-permute-start.46 = (bf16[512,1536]{1,0:T(8,128)(2,1)S(1)}, bf16[512,1536]{1,0:T(8,128)(2,1)S(1)}, u32[]{:S(2)}, u32[]{:S(2)}) collective-permute-start(bf16[512,1536]{1,0:T(8,128)(2,1)S(1)} %get-tuple-element.619), channel_id=1, source_target_pairs={{0,1},{1,0},{2,3},{3,2},{4,5},{5,4},{6,7},{7,6},{8,9},{9,8},{10,11... | collective-permute-start | bytes 4718600 | tf_op jit(solution)/shard_map/ppermute | solution.py:35
  317.5 30.1 %collective-permute-start.47 = (bf16[96,6144]{1,0:T(8,128)(2,1)S(1)}, bf16[96,6144]{1,0:T(8,128)(2,1)S(1)}, u32[]{:S(2)}, u32[]{:S(2)}) collective-permute-start(bf16[96,6144]{1,0:T(8,128)(2,1)S(1)} %get-tuple-element.626), channel_id=1, source_target_pairs={{0,8},{2,10},{8,16},{10,18},{16,24},{18,26},{24,28},{26,30},{28,20... | collective-permute-start | bytes 3538952 | tf_op jit(solution)/shard_map/ppermute | solution.py:213
  318.1 29.5 %collective-permute-start.48 = (bf16[96,6144]{1,0:T(8,128)(2,1)S(1)}, bf16[96,6144]{1,0:T(8,128)(2,1)S(1)}, u32[]{:S(2)}, u32[]{:S(2)}) collective-permute-start(bf16[96,6144]{1,0:T(8,128)(2,1)S(1)} %get-tuple-element.627), channel_id=1, source_target_pairs={{8,0},{10,2},{16,8},{18,10},{24,16},{26,18},{28,24},{30,26},{20,28... | collective-permute-start | bytes 3538952 | tf_op jit(solution)/shard_map/ppermute | solution.py:214
  352.1 27.3 %collective-permute-start.49 = (bf16[96,6144]{1,0:T(8,128)(2,1)}, bf16[96,6144]{1,0:T(8,128)(2,1)S(1)}, u32[]{:S(2)}, u32[]{:S(2)}) collective-permute-start(bf16[96,6144]{1,0:T(8,128)(2,1)} %get-tuple-element.650), channel_id=1, source_target_pairs={{0,8},{2,10},{8,16},{10,18},{16,24},{18,26},{24,28},{26,30},{28,20... | collective-permute-start | bytes 3538952 | tf_op jit(solution)/shard_map/ppermute | solution.py:213
  352.7 27.2 %collective-permute-start.50 = (bf16[96,6144]{1,0:T(8,128)(2,1)}, bf16[96,6144]{1,0:T(8,128)(2,1)}, u32[]{:S(2)}, u32[]{:S(2)}) collective-permute-start(bf16[96,6144]{1,0:T(8,128)(2,1)} %get-tuple-element.651), channel_id=1, source_target_pairs={{8,0},{10,2},{16,8},{18,10},{24,16},{26,18},{28,24},{30,26},{20,28... | collective-permute-start | bytes 3538952 | tf_op jit(solution)/shard_map/ppermute | solution.py:214
  356.1 32.9 %collective-permute-start.53 = (bf16[512,1536]{1,0:T(8,128)(2,1)}, bf16[512,1536]{1,0:T(8,128)(2,1)}, u32[]{:S(2)}, u32[]{:S(2)}) collective-permute-start(bf16[512,1536]{1,0:T(8,128)(2,1)} %get-tuple-element.702), channel_id=1, source_target_pairs={{0,1},{1,0},{2,3},{3,2},{4,5},{5,4},{6,7},{7,6},{8,9},{9,8},{10,11... | collective-permute-start | bytes 4718600 | tf_op jit(solution)/shard_map/ppermute | solution.py:35
  369.6 14.6 %collective-permute-start.51 = (bf16[96,1152]{1,0:T(8,128)(2,1)S(1)}, bf16[96,1152]{1,0:T(8,128)(2,1)S(1)}, u32[]{:S(2)}, u32[]{:S(2)}) collective-permute-start(bf16[96,1152]{1,0:T(8,128)(2,1)S(1)} %get-tuple-element.658), channel_id=1, source_target_pairs={{0,8},{2,10},{8,16},{10,18},{16,24},{18,26},{24,28},{26,30},{28,20... | collective-permute-start | bytes 663560 | tf_op jit(solution)/shard_map/ppermute | solution.py:213
  370.2 14.0 %collective-permute-start.52 = (bf16[96,1152]{1,0:T(8,128)(2,1)S(1)}, bf16[96,1152]{1,0:T(8,128)(2,1)S(1)}, u32[]{:S(2)}, u32[]{:S(2)}) collective-permute-start(bf16[96,1152]{1,0:T(8,128)(2,1)S(1)} %get-tuple-element.659), channel_id=1, source_target_pairs={{8,0},{10,2},{16,8},{18,10},{24,16},{26,18},{28,24},{30,26},{20,28... | collective-permute-start | bytes 663560 | tf_op jit(solution)/shard_map/ppermute | solution.py:214
  398.5 11.7 %collective-permute-start.56 = (bf16[96,2304]{1,0:T(8,128)(2,1)}, bf16[96,2304]{1,0:T(8,128)(2,1)S(1)}, u32[]{:S(2)}, u32[]{:S(2)}) collective-permute-start(bf16[96,2304]{1,0:T(8,128)(2,1)} %get-tuple-element.677), channel_id=1, source_target_pairs={{0,8},{2,10},{8,16},{10,18},{16,24},{18,26},{24,28},{26,30},{28,20... | collective-permute-start | bytes 1327112 | tf_op jit(solution)/shard_map/ppermute | solution.py:213
  398.6 11.6 %collective-permute-start.57 = (bf16[96,2304]{1,0:T(8,128)(2,1)}, bf16[96,2304]{1,0:T(8,128)(2,1)S(1)}, u32[]{:S(2)}, u32[]{:S(2)}) collective-permute-start(bf16[96,2304]{1,0:T(8,128)(2,1)} %get-tuple-element.678), channel_id=1, source_target_pairs={{8,0},{10,2},{16,8},{18,10},{24,16},{26,18},{28,24},{30,26},{20,28... | collective-permute-start | bytes 1327112 | tf_op jit(solution)/shard_map/ppermute | solution.py:214
  (80 other events, 779.1 us)
